TPU v7x, 512 devices: a whole 4x4x16 slice. The times are simulated.
512 devices in a mesh: dp: 4 (over x), expert: 128 (over z, y, core).
Axes of the slice: x: 4, y: 4, z: 16, core: 2. Of those that a mesh axis runs over, the one named last changes fastest.
Arguments:
- tokens: bfloat16 [65536, 2048], P(('dp', 'expert')), may hold values from -6 to 6
- hidden_grad: bfloat16 [65536, 1, 768], P(('dp', 'expert')), may hold values from -6 to 6
- gate_prob: float32 [65536, 1], P(('dp', 'expert')), may hold values from 0.2 to 1
- slot_choice: int32 [65536, 1], P(('dp', 'expert')), may hold values from 0 to 127; in each aligned block of 128 rows (0 to 127, 128 to 255, ...) at most 2 rows name the same one
- replica_plan: int32 [128], replicated, may hold values from 0 to 63, as said below
- weights: bfloat16 [64, 2, 2048, 768], P(None, None, ('dp', 'expert')), may hold values from -0.125 to 0.125
Outputs:
- input_grad: bfloat16 [65536, 2048], P(('dp', 'expert'))
- expert_grad: bfloat16 [64, 2, 2048, 768], P(None, None, ('dp', 'expert'))
Inputs may be any that keep to these rules, and one draw needn't show every extreme that they name: `slot_choice`: among the tokens of one device no slot is named more than 2 times, and 2 is reached; the picks of one token name different slots. `replica_plan`: every expert is held by at least one slot.
All inputs are finite; a program needn't handle non-finite values.
Results may differ from a plain program's by a relative error of at most 0.007.
Values may be sent and summed in bfloat16 or wider, within the bound.
A program may use at most 64 MiB of HBM per device.

v0:
```python
import jax
import jax.numpy as jnp
from jax import lax
from jax.sharding import PartitionSpec as P


def back_project(grad_gate, grad_up, weight_pair):
    contract_cols = (((1,), (1,)), ((), ()))
    first_term = lax.dot_general(
        grad_gate, weight_pair[0], contract_cols, preferred_element_type=jnp.float32
    )
    return first_term + lax.dot_general(
        grad_up, weight_pair[1], contract_cols, preferred_element_type=jnp.float32
    )


def row_products(inputs, grad_gate, grad_up):
    contract_rows = (((0,), (0,)), ((), ()))
    return jnp.stack(
        [
            lax.dot_general(inputs, grad_gate, contract_rows, preferred_element_type=jnp.float32),
            lax.dot_general(inputs, grad_up, contract_rows, preferred_element_type=jnp.float32),
        ]
    )


def per_device(tokens, hidden_grad, gate_prob, slot_choice, replica_plan, weights):
    expert_count = lax.axis_size("expert")
    group_count = lax.axis_size("dp")
    token_count, pick_count = slot_choice.shape
    row_count = token_count * pick_count
    capacity = max(2, 2 * row_count // expert_count)
    depth_rows = expert_count * capacity
    model_width = tokens.shape[1]
    hidden_width = hidden_grad.shape[2]
    expert_total = weights.shape[0]
    shard_rows = weights.shape[2]
    block_rows = shard_rows * expert_count
    flat_slot = slot_choice.reshape(row_count)
    slot_member = (flat_slot[:, None] == jnp.arange(expert_count, dtype=jnp.int32)[None, :]).astype(
        jnp.int32
    )
    ranking = jnp.sum((jnp.cumsum(slot_member, axis=0) - 1) * slot_member, axis=1)
    position = flat_slot * capacity + ranking
    scatter_table = (jnp.arange(depth_rows, dtype=jnp.int32)[:, None] == position[None, :]).astype(
        jnp.bfloat16
    )
    token_rows = jnp.repeat(tokens, pick_count, axis=0)
    cotangent = (gate_prob[:, :, None] * hidden_grad.astype(jnp.float32)).astype(jnp.bfloat16)
    cotangent = cotangent.reshape(row_count, hidden_width)
    send_inputs = jnp.dot(scatter_table, token_rows, preferred_element_type=jnp.float32).astype(
        jnp.bfloat16
    )
    send_cotangent = jnp.dot(scatter_table, cotangent, preferred_element_type=jnp.float32).astype(
        jnp.bfloat16
    )
    recv_inputs, recv_cotangent = (
        lax.all_to_all(
            send_inputs.reshape(expert_count, capacity, model_width),
            "expert",
            split_axis=0,
            concat_axis=0,
            tiled=True,
        ),
        lax.all_to_all(
            send_cotangent.reshape(expert_count, capacity, hidden_width),
            "expert",
            split_axis=0,
            concat_axis=0,
            tiled=True,
        ),
    )
    recv_inputs = recv_inputs.reshape(depth_rows, model_width)
    recv_cotangent = recv_cotangent.reshape(depth_rows, hidden_width)
    chooser = (replica_plan[:, None] == jnp.arange(expert_total, dtype=jnp.int32)[None, :]).astype(
        jnp.bfloat16
    )
    send_weights = jnp.einsum(
        "se,ekdf->skdf", chooser, weights, preferred_element_type=jnp.float32
    ).astype(jnp.bfloat16)
    own_weights = lax.all_to_all(
        send_weights, "expert", split_axis=0, concat_axis=2, tiled=True
    ).reshape(2, block_rows, hidden_width)
    piece = lax.all_gather(own_weights, "dp", axis=1, tiled=True)
    gate_sum = jnp.dot(recv_inputs, piece[0], preferred_element_type=jnp.float32)
    up_sum = jnp.dot(recv_inputs, piece[1], preferred_element_type=jnp.float32)
    sigma = jax.nn.sigmoid(gate_sum)
    scaled = recv_cotangent.astype(jnp.float32)
    grad_gate = (scaled * up_sum * sigma * (1.0 + gate_sum * (1.0 - sigma))).astype(jnp.bfloat16)
    grad_up = (scaled * gate_sum * sigma).astype(jnp.bfloat16)
    all_gate, all_up = (
        lax.all_gather(grad_gate, "dp", axis=0, tiled=True),
        lax.all_gather(grad_up, "dp", axis=0, tiled=True),
    )
    split_inputs = recv_inputs.reshape(depth_rows, group_count, block_rows)
    all_columns = lax.all_to_all(
        split_inputs, "dp", split_axis=1, concat_axis=0, tiled=True
    ).reshape(group_count * depth_rows, block_rows)
    row_terms = back_project(all_gate, all_up, own_weights).astype(jnp.bfloat16)
    summed = jnp.zeros((2, block_rows, hidden_width), jnp.float32)
    for group_index in range(group_count):
        lower = group_index * depth_rows
        upper = lower + depth_rows
        products = row_products(
            all_columns[lower:upper], all_gate[lower:upper], all_up[lower:upper]
        )
        summed = summed + lax.optimization_barrier(products.astype(jnp.bfloat16)).astype(
            jnp.float32
        )
    pieces = summed.reshape(2, expert_count, shard_rows, hidden_width)
    gathered = lax.all_to_all(
        pieces.astype(jnp.bfloat16), "expert", split_axis=1, concat_axis=1, tiled=True
    ).astype(pieces.dtype)
    membership = (
        jnp.arange(expert_total, dtype=jnp.int32)[:, None] == replica_plan[None, :]
    ).astype(jnp.float32)
    expert_grad = jnp.einsum("es,ksdf->ekdf", membership, gathered, precision=lax.Precision.HIGHEST)
    expert_grad = (expert_grad / group_count).astype(jnp.bfloat16)
    joined = lax.all_to_all(
        row_terms.reshape(group_count, depth_rows, block_rows),
        "dp",
        split_axis=0,
        concat_axis=2,
        tiled=True,
    )
    back_rows = lax.all_to_all(
        joined.reshape(expert_count, capacity, model_width),
        "expert",
        split_axis=0,
        concat_axis=0,
        tiled=True,
    )
    back_rows = back_rows.reshape(depth_rows, model_width)
    token_grads = lax.dot_general(
        scatter_table, back_rows, (((0,), (0,)), ((), ())), preferred_element_type=jnp.float32
    )
    input_grad = jnp.sum(token_grads.reshape(token_count, pick_count, model_width), axis=1).astype(
        jnp.bfloat16
    )
    return (input_grad, expert_grad)


def solution(mesh):
    placed = (
        P(("dp", "expert"), None),
        P(("dp", "expert"), None, None),
        P(("dp", "expert"), None),
        P(("dp", "expert"), None),
        P(),
        P(None, None, ("dp", "expert"), None),
    )
    return jax.shard_map(
        per_device,
        mesh=mesh,
        in_specs=placed,
        out_specs=(P(("dp", "expert"), None), P(None, None, ("dp", "expert"), None)),
        check_vma=False,
    )
```

profile of v0, /device:TPU:1, one launch (start us, length us, event | category | flops | bytes accessed | tf_op | source)
XLA Modules:
  0.0 491.3 jit_solution(11595988162404496423)
XLA Ops:
  10.8 93.3 %all_to_all.65 = bf16[128,2,4,768]{3,2,1,0:T(4,128)(2,1)S(1)} all-to-all(bf16[128,2,4,768]{3,2,1,0:T(4,128)(2,1)S(1)} %copy.26), channel_id=1, replica_groups=mesh['dp'=4,'expert'=128] {'expert'}, dimensions={0} | all-to-all | bytes 3145728 | tf_op jit(solution)/shard_map/all_to_all | solution.py:81
  104.1 2.4 copy.27
  108.9 11.6 %all-to-all-start = ((bf16[128,2,768]{2,1,0:T(2,128)(2,1)}), bf16[128,2,768]{2,1,0:T(2,128)(2,1)S(1)}, u32[]{:S(2)}, u32[]{:S(2)}) async-start(bf16[128,2,768]{2,1,0:T(2,128)(2,1)} %reshape.66), calls=%async_computation | async-start | bytes 786432 | tf_op jit(solution)/shard_map/all_to_all | solution.py:65
  123.6 22.3 %all-to-all-done = bf16[128,2,768]{2,1,0:T(2,128)(2,1)S(1)} async-done(((bf16[128,2,768]{2,1,0:T(2,128)(2,1)}), bf16[128,2,768]{2,1,0:T(2,128)(2,1)S(1)}, u32[]{:S(2)}, u32[]{:S(2)}) %all-to-all-start) | async-done | bytes 393248 | tf_op jit(solution)/shard_map/all_to_all | solution.py:65
  145.9 8.9 %all-to-all-start.1 = ((bf16[128,2,2048]{2,1,0:T(2,128)(2,1)}), bf16[128,2,2048]{2,1,0:T(2,128)(2,1)S(1)}, u32[]{:S(2)}, u32[]{:S(2)}) async-start(bf16[128,2,2048]{2,1,0:T(2,128)(2,1)} %reshape.67), calls=%async_computation.1 | async-start | bytes 2097152 | tf_op jit(solution)/shard_map/all_to_all | solution.py:58
  156.0 50.9 %all-to-all-done.1 = bf16[128,2,2048]{2,1,0:T(2,128)(2,1)S(1)} async-done(((bf16[128,2,2048]{2,1,0:T(2,128)(2,1)}), bf16[128,2,2048]{2,1,0:T(2,128)(2,1)S(1)}, u32[]{:S(2)}, u32[]{:S(2)}) %all-to-all-start.1) | async-done | bytes 1048608 | tf_op jit(solution)/shard_map/all_to_all | solution.py:58
  208.2 12.7 %fusion.40 = (bf16[1,2048,768]{2,0,1:T(2,128)(2,1)S(1)}, bf16[1,2048,768]{2,0,1:T(2,128)(2,1)S(1)}) fusion(bf16[2,2048,768]{2,0,1:T(2,128)(2,1)} %all-gather.4.cloned.1.call-done), kind=kLoop, calls=%fused_computation.69 | loop fusion | bytes 12582912 | tf_op jit(solution)/shard_map/slice | solution.py:85
  228.5 24.9 %all-gather.6.cloned.1.call-done = bf16[1024,768]{1,0:T(8,128)(2,1)} async-done(((bf16[256,768]{1,0:T(8,128)(2,1)}), bf16[1024,768]{1,0:T(8,128)(2,1)}) %all-gather.6.cloned.1.call-update) | async-done | bytes 1572880 | tf_op jit(solution)/shard_map/all_gather | solution.py:92
  253.4 3.8 fusion.42
  257.2 33.1 %all-gather.8.cloned.1.call-done = bf16[1024,768]{1,0:T(8,128)(2,1)} async-done(((bf16[256,768]{1,0:T(8,128)(2,1)}), bf16[1024,768]{1,0:T(8,128)(2,1)}) %all-gather.8.cloned.1.call-update) | async-done | bytes 1572880 | tf_op jit(solution)/shard_map/all_gather | solution.py:93
  290.3 4.1 add_convert_fusion.1
  294.4 3.5 all-to-all-start.3
  299.4 2.4 copy.31
  301.8 10.4 %all-to-all-done.3 = bf16[4,256,512]{2,1,0:T(8,128)(2,1)S(1)} async-done(((bf16[4,256,512]{2,1,0:T(8,128)(2,1)}), bf16[4,256,512]{2,1,0:T(8,128)(2,1)S(1)}, u32[]{:S(2)}, u32[]{:S(2)}) %all-to-all-start.3) | async-done | bytes 1048608 | tf_op jit(solution)/shard_map/all_to_all | solution.py:119
  312.2 3.5 all-to-all-start.5
  317.5 2.3 reshape.71
  319.8 9.4 %all-to-all-done.5 = bf16[256,4,512]{2,0,1:T(8,128)(2,1)S(1)} async-done(((bf16[256,4,512]{2,0,1:T(8,128)(2,1)}), bf16[256,4,512]{2,0,1:T(8,128)(2,1)S(1)}, u32[]{:S(2)}, u32[]{:S(2)}) %all-to-all-start.5) | async-done | bytes 1048608 | tf_op jit(solution)/shard_map/all_to_all | solution.py:96
  329.2 18.5 %all-to-all-start.4 = ((bf16[128,2,2048]{2,1,0:T(2,128)(2,1)}), bf16[128,2,2048]{2,1,0:T(2,128)(2,1)S(1)}, u32[]{:S(2)}, u32[]{:S(2)}) async-start(bf16[128,2,2048]{2,1,0:T(2,128)(2,1)} %reshape.71), calls=%async_computation.4 | async-start | bytes 2097152 | tf_op jit(solution)/shard_map/all_to_all | solution.py:126
  355.0 2.0 add_convert_fusion
  356.9 2.9 convert_element_type.82
  361.5 38.3 %all-to-all-done.4 = bf16[128,2,2048]{2,1,0:T(2,128)(2,1)S(1)} async-done(((bf16[128,2,2048]{2,1,0:T(2,128)(2,1)}), bf16[128,2,2048]{2,1,0:T(2,128)(2,1)S(1)}, u32[]{:S(2)}, u32[]{:S(2)}) %all-to-all-start.4) | async-done | bytes 1048608 | tf_op jit(solution)/shard_map/all_to_all | solution.py:126
  399.8 10.0 %all-to-all-start.6 = ((bf16[2,128,4,768]{3,2,0,1:T(4,128)(2,1)}), bf16[2,128,4,768]{3,2,0,1:T(4,128)(2,1)S(1)}, u32[]{:S(2)}, u32[]{:S(2)}) async-start(bf16[2,128,4,768]{3,2,0,1:T(4,128)(2,1)} %copy.32), calls=%async_computation.6 | async-start | bytes 3145728 | tf_op jit(solution)/shard_map/all_to_all | solution.py:111
  411.1 2.4 convolution_convert_fusion.1
  413.5 69.3 %all-to-all-done.6 = bf16[2,128,4,768]{3,2,0,1:T(4,128)(2,1)S(1)} async-done(((bf16[2,128,4,768]{3,2,0,1:T(4,128)(2,1)}), bf16[2,128,4,768]{3,2,0,1:T(4,128)(2,1)S(1)}, u32[]{:S(2)}, u32[]{:S(2)}) %all-to-all-start.6) | async-done | bytes 1572896 | tf_op jit(solution)/shard_map/all_to_all | solution.py:111
  (62 shorter events, 34.4 us)
Async XLA Ops:
  7.2 1.1 copy-start
  7.2 201.0 %all-gather.4.cloned.1.call-start = ((), (), s32[]{:S(2)}) async-start(), calls=%async_computation.7 | async-start | bytes 7864320 | tf_op jit(solution)/shard_map/all_gather | solution.py:84
  106.5 0.7 copy-start.7
  106.5 1.1 copy-start.6
  106.5 1.1 copy-start.9
  108.9 37.0 %all-to-all-start = ((bf16[128,2,768]{2,1,0:T(2,128)(2,1)}), bf16[128,2,768]{2,1,0:T(2,128)(2,1)S(1)}, u32[]{:S(2)}, u32[]{:S(2)}) async-start(bf16[128,2,768]{2,1,0:T(2,128)(2,1)} %reshape.66), calls=%async_computation | async-start | bytes 786432 | tf_op jit(solution)/shard_map/all_to_all | solution.py:65
  145.9 61.0 %all-to-all-start.1 = ((bf16[128,2,2048]{2,1,0:T(2,128)(2,1)}), bf16[128,2,2048]{2,1,0:T(2,128)(2,1)S(1)}, u32[]{:S(2)}, u32[]{:S(2)}) async-start(bf16[128,2,2048]{2,1,0:T(2,128)(2,1)} %reshape.67), calls=%async_computation.1 | async-start | bytes 2097152 | tf_op jit(solution)/shard_map/all_to_all | solution.py:58
  154.8 98.6 %all-gather.6.cloned.1.call-start = ((), (), s32[]{:S(2)}) async-start(), calls=%async_computation.8 | async-start | bytes 1966080 | tf_op jit(solution)/shard_map/all_gather | solution.py:92
  208.2 12.7 %copy-start.5 = (f32[256,768]{1,0:T(8,128)S(1)}, f32[256,768]{1,0:T(8,128)}, u32[]{:S(2)}) copy-start(f32[256,768]{1,0:T(8,128)} %reshape.73) | copy-start | bytes 2359300
  208.2 12.7 %copy-start.4 = (bf16[256,2048]{1,0:T(8,128)(2,1)S(1)}, bf16[256,2048]{1,0:T(8,128)(2,1)}, u32[]{:S(2)}) copy-start(bf16[256,2048]{1,0:T(8,128)(2,1)} %reshape.68) | copy-start | bytes 3145732
  224.6 65.7 %all-gather.8.cloned.1.call-start = ((), (), s32[]{:S(2)}) async-start(), calls=%async_computation.9 | async-start | bytes 1966080 | tf_op jit(solution)/shard_map/all_gather | solution.py:93
  294.4 17.8 %all-to-all-start.3 = ((bf16[4,256,512]{2,1,0:T(8,128)(2,1)}), bf16[4,256,512]{2,1,0:T(8,128)(2,1)S(1)}, u32[]{:S(2)}, u32[]{:S(2)}) async-start(bf16[4,256,512]{2,1,0:T(8,128)(2,1)} %bitcast.99), calls=%async_computation.3 | async-start | bytes 2097152 | tf_op jit(solution)/shard_map/all_to_all | solution.py:119
  312.2 17.0 %all-to-all-start.5 = ((bf16[256,4,512]{2,0,1:T(8,128)(2,1)}), bf16[256,4,512]{2,0,1:T(8,128)(2,1)S(1)}, u32[]{:S(2)}, u32[]{:S(2)}) async-start(bf16[256,4,512]{2,0,1:T(8,128)(2,1)} %copy.31), calls=%async_computation.5 | async-start | bytes 2097152 | tf_op jit(solution)/shard_map/all_to_all | solution.py:96
  329.2 70.6 %all-to-all-start.4 = ((bf16[128,2,2048]{2,1,0:T(2,128)(2,1)}), bf16[128,2,2048]{2,1,0:T(2,128)(2,1)S(1)}, u32[]{:S(2)}, u32[]{:S(2)}) async-start(bf16[128,2,2048]{2,1,0:T(2,128)(2,1)} %reshape.71), calls=%async_computation.4 | async-start | bytes 2097152 | tf_op jit(solution)/shard_map/all_to_all | solution.py:126
  350.6 1.4 copy-start.2
  350.6 1.9 copy-start.3
  399.8 83.0 %all-to-all-start.6 = ((bf16[2,128,4,768]{3,2,0,1:T(4,128)(2,1)}), bf16[2,128,4,768]{3,2,0,1:T(4,128)(2,1)S(1)}, u32[]{:S(2)}, u32[]{:S(2)}) async-start(bf16[2,128,4,768]{3,2,0,1:T(4,128)(2,1)} %copy.32), calls=%async_computation.6 | async-start | bytes 3145728 | tf_op jit(solution)/shard_map/all_to_all | solution.py:111
  409.8 73.0 %copy-start.8 = (s32[128]{0:T(128)S(1)}, s32[128]{0:T(128)}, u32[]{:S(2)}) copy-start(s32[128]{0:T(128)} %param.10) | copy-start | bytes 1540
  411.1 73.7 %copy-start.1 = (bf16[64,2,4,768]{3,2,1,0:T(4,128)(2,1)S(1)}, bf16[64,2,4,768]{3,2,1,0:T(4,128)(2,1)}, u32[]{:S(2)}) copy-start(bf16[64,2,4,768]{3,2,1,0:T(4,128)(2,1)} %param.11) | copy-start | bytes 2359300
Sparse Core Ops, SparseCore 0:
  106.7 69.4 all-gather.3
  224.7 28.6 all-gather.5
  256.1 34.1 all-gather.7
where the time goes:
time: 496 us; the launch traced here: 491 us
  waiting for transfers between devices  259 us (52%)
  blocking collectives  93.3 us (19%)
  starting transfers between devices  56.4 us (11%)
  local copies, waits for them, and re-layouts  42.5 us (9%)
  matrix products  22.8 us (5%)
  between operations  14 us (3%)
    all_to_all x1, blocking collectives, per_device(): lax.all_to_all(send_weights, 'expert', split_axis=0, concat_axis=2, tiled...  93.3 us
    all_to_all x1, waiting for transfers between devices, per_device(): lax.all_to_all(pieces.astype(jnp.bfloat16), 'expert', split_axis=1, conca...  69.3 us
    all_to_all x1, waiting for transfers between devices, per_device(): lax.all_to_all(send_inputs.reshape(expert_count, capacity, model_width),...  50.9 us
    all_to_all x1, waiting for transfers between devices, per_device(): lax.all_to_all(joined.reshape(expert_count, capacity, model_width), 'expe...  38.3 us
    all_gather x1, waiting for transfers between devices, per_device(): lax.all_gather(grad_up, 'dp', axis=0, tiled=True)  33.1 us
    all_gather x1, waiting for transfers between devices, per_device(): lax.all_gather(grad_gate, 'dp', axis=0, tiled=True)  24.9 us
    all_to_all x1, waiting for transfers between devices, per_device(): lax.all_to_all(send_cotangent.reshape(expert_count, capacity, hidden_widt...  22.3 us
    all_to_all x1, starting transfers between devices, per_device(): lax.all_to_all(joined.reshape(expert_count, capacity, model_width), 'expe...  18.5 us
  transfers between devices with their start and end apart: 9, of which 8 were waited for; matrix products, arithmetic and copies ran while one was open for 8% of the time, Pallas kernels for 0%

commit v1 on v0

v1 whole, which is shorter than its diff:
```python
import jax
import jax.numpy as jnp
from jax import lax
from jax.sharding import PartitionSpec as P


def per_device(tokens, hidden_grad, gate_prob, slot_choice, replica_plan, weights):
    expert_count = lax.axis_size("expert")
    group_count = lax.axis_size("dp")
    token_count, pick_count = slot_choice.shape
    row_count = token_count * pick_count
    capacity = max(2, 2 * row_count // expert_count)
    depth_rows = expert_count * capacity
    model_width = tokens.shape[1]
    hidden_width = hidden_grad.shape[2]
    expert_total = weights.shape[0]
    shard_rows = weights.shape[2]
    block_rows = shard_rows * expert_count

    chooser = (replica_plan[:, None] == jnp.arange(expert_total, dtype=jnp.int32)[None, :]).astype(
        jnp.bfloat16
    )
    send_weights = jnp.einsum(
        "se,ekdf->skdf", chooser, weights, preferred_element_type=jnp.float32
    ).astype(jnp.bfloat16)
    own_weights = lax.all_to_all(send_weights, "expert", split_axis=0, concat_axis=0, tiled=True)
    own_weights = own_weights.transpose(1, 0, 2, 3).reshape(2, block_rows, hidden_width)
    piece = lax.all_gather(own_weights, "dp", axis=0, tiled=False)

    flat_slot = slot_choice.reshape(row_count)
    slot_member = (flat_slot[:, None] == jnp.arange(expert_count, dtype=jnp.int32)[None, :]).astype(
        jnp.int32
    )
    ranking = jnp.sum((jnp.cumsum(slot_member, axis=0) - 1) * slot_member, axis=1)
    position = flat_slot * capacity + ranking
    scatter_table = (jnp.arange(depth_rows, dtype=jnp.int32)[:, None] == position[None, :]).astype(
        jnp.bfloat16
    )
    token_rows = jnp.repeat(tokens, pick_count, axis=0)
    cotangent = (gate_prob[:, :, None] * hidden_grad.astype(jnp.float32)).astype(jnp.bfloat16)
    cotangent = cotangent.reshape(row_count, hidden_width)
    routed = jnp.concatenate([token_rows, cotangent], axis=1)
    send_rows = jnp.dot(scatter_table, routed, preferred_element_type=jnp.float32).astype(
        jnp.bfloat16
    )
    recv_rows = lax.all_to_all(
        send_rows.reshape(expert_count, capacity, model_width + hidden_width),
        "expert",
        split_axis=0,
        concat_axis=0,
        tiled=True,
    ).reshape(depth_rows, model_width + hidden_width)
    recv_inputs = recv_rows[:, :model_width]
    recv_cotangent = recv_rows[:, model_width:]

    column_blocks = jnp.stack(
        [recv_inputs[:, k * block_rows : (k + 1) * block_rows] for k in range(group_count)]
    )
    all_columns = lax.all_to_all(
        column_blocks, "dp", split_axis=0, concat_axis=0, tiled=True
    ).reshape(group_count * depth_rows, block_rows)

    gate_sum = jnp.zeros((depth_rows, hidden_width), jnp.float32)
    up_sum = jnp.zeros((depth_rows, hidden_width), jnp.float32)
    for k in range(group_count):
        block = recv_inputs[:, k * block_rows : (k + 1) * block_rows]
        gate_sum = gate_sum + jnp.dot(block, piece[k, 0], preferred_element_type=jnp.float32)
        up_sum = up_sum + jnp.dot(block, piece[k, 1], preferred_element_type=jnp.float32)
    sigma = jax.nn.sigmoid(gate_sum)
    scaled = recv_cotangent.astype(jnp.float32)
    grad_gate = (scaled * up_sum * sigma * (1.0 + gate_sum * (1.0 - sigma))).astype(jnp.bfloat16)
    grad_up = (scaled * gate_sum * sigma).astype(jnp.bfloat16)
    grads = jnp.concatenate([grad_gate, grad_up], axis=1)
    all_grads = lax.all_gather(grads, "dp", axis=0, tiled=True)

    contract_cols = (((1,), (1,)), ((), ()))
    row_terms = jnp.concatenate(
        [
            (
                lax.dot_general(
                    grad_gate, piece[k, 0], contract_cols, preferred_element_type=jnp.float32
                )
                + lax.dot_general(
                    grad_up, piece[k, 1], contract_cols, preferred_element_type=jnp.float32
                )
            ).astype(jnp.bfloat16)
            for k in range(group_count)
        ],
        axis=1,
    )
    back_rows = lax.all_to_all(
        row_terms.reshape(expert_count, capacity, model_width),
        "expert",
        split_axis=0,
        concat_axis=0,
        tiled=True,
    ).reshape(depth_rows, model_width)

    summed = lax.dot_general(
        all_columns, all_grads, (((0,), (0,)), ((), ())), preferred_element_type=jnp.float32
    ).astype(jnp.bfloat16)
    pieces = summed.reshape(expert_count, shard_rows, 2, hidden_width).transpose(0, 2, 1, 3)
    gathered = lax.all_to_all(pieces, "expert", split_axis=0, concat_axis=0, tiled=True)
    membership = (
        jnp.arange(expert_total, dtype=jnp.int32)[:, None] == replica_plan[None, :]
    ).astype(jnp.bfloat16)
    expert_grad = jnp.einsum(
        "es,skdf->ekdf", membership, gathered, preferred_element_type=jnp.float32
    )
    expert_grad = (expert_grad / group_count).astype(jnp.bfloat16)

    token_grads = lax.dot_general(
        scatter_table, back_rows, (((0,), (0,)), ((), ())), preferred_element_type=jnp.float32
    )
    input_grad = jnp.sum(token_grads.reshape(token_count, pick_count, model_width), axis=1).astype(
        jnp.bfloat16
    )
    return (input_grad, expert_grad)


def solution(mesh):
    placed = (
        P(("dp", "expert"), None),
        P(("dp", "expert"), None, None),
        P(("dp", "expert"), None),
        P(("dp", "expert"), None),
        P(),
        P(None, None, ("dp", "expert"), None),
    )
    return jax.shard_map(
        per_device,
        mesh=mesh,
        in_specs=placed,
        out_specs=(P(("dp", "expert"), None), P(None, None, ("dp", "expert"), None)),
        check_vma=False,
    )
```

time: 496 us -> 381 us (0.77)
  waiting for transfers between devices: 259 us -> 111 us
  blocking collectives: 93.3 us -> 173 us
  starting transfers between devices: 56.4 us -> 25.4 us
  local copies, waits for them, and re-layouts: 42.5 us -> 19.6 us
  matrix products: 22.8 us -> 30.3 us
    all_to_all x6 -> x3, waiting for transfers between devices: 201 us -> 92.7 us  [the longest x1 69.4 us: per_device(): lax.all_to_all(pieces, 'expert', split_axis=0, concat_axis=0, tiled=True)]
    all_to_all x1 -> x2, blocking collectives: 93.3 us -> 173 us  [the longest x1 93.3 us: per_device(): lax.all_to_all(send_weights, 'expert', split_axis=0, concat_axis=0, tiled...]
    all_gather x3 -> x2, waiting for transfers between devices: 58 us -> 18.2 us  [the longest x1 18.1 us: per_device(): all_grads = lax.all_gather(grads, 'dp', axis=0, tiled=True)]
    all_to_all x6 -> x3, starting transfers between devices: 56.1 us -> 25.1 us  [the longest x1 10.9 us: per_device(): lax.all_to_all(row_terms.reshape(expert_count, capacity, model_width), 'e...]
    slice x2 -> x0, local copies, waits for them, and re-layouts: 14.1 us -> none  [the longest x1 12.7 us: per_device(): piece[0]]
    dot_general x15 -> x19, matrix products: 19.1 us -> 26.7 us  [the longest x4 6.13 us: per_device(): lax.dot_general(grad_up, piece[k, 1], contract_cols, preferred_element_ty...]
    reshape x5 -> x6, local copies, waits for them, and re-layouts: 7.24 us -> 13.1 us  [the longest x2 5.42 us: per_device(): summed.reshape(expert_count, shard_rows, 2, hidden_width)]
    convert_element_type x3 -> x0, local copies, waits for them, and re-layouts: 5.6 us -> none  [the longest x2 4.61 us: per_device(): pieces.astype(jnp.bfloat16)]
  transfers between devices with their start and end apart: 9 -> 5, of which waited for: 8 -> 3; matrix products, arithmetic and copies ran while one was open for 8% -> 12% of each run, Pallas kernels for 0% -> 0%
where the time goes in v1:
time: 381 us; the launch traced here: 376 us
  blocking collectives  173 us (45%)
  waiting for transfers between devices  111 us (29%)
  matrix products  30.3 us (8%)
  starting transfers between devices  25.4 us (7%)
  local copies, waits for them, and re-layouts  19.6 us (5%)
  between operations  14.4 us (4%)
    all_to_all x1, blocking collectives, per_device(): lax.all_to_all(send_weights, 'expert', split_axis=0, concat_axis=0, tiled...  93.3 us
    all_to_all x1, blocking collectives, per_device(): lax.all_to_all(send_rows.reshape(expert_count, capacity, model_width + hi...  79.7 us
    all_to_all x1, waiting for transfers between devices, per_device(): lax.all_to_all(pieces, 'expert', split_axis=0, concat_axis=0, tiled=True)  69.4 us
    all_to_all x1, waiting for transfers between devices, per_device(): lax.all_to_all(row_terms.reshape(expert_count, capacity, model_width), 'e...  23.3 us
    all_gather x1, waiting for transfers between devices, per_device(): all_grads = lax.all_gather(grads, 'dp', axis=0, tiled=True)  18.1 us
    all_to_all x1, starting transfers between devices, per_device(): lax.all_to_all(row_terms.reshape(expert_count, capacity, model_width), 'e...  10.9 us
    all_to_all x1, starting transfers between devices, per_device(): lax.all_to_all(pieces, 'expert', split_axis=0, concat_axis=0, tiled=True)  9.99 us
  transfers between devices with their start and end apart: 5, of which 3 were waited for; matrix products, arithmetic and copies ran while one was open for 12% of the time, Pallas kernels for 0%

profile of v1, /device:TPU:1, one launch (start us, length us, event | category | flops | bytes accessed | tf_op | source)
XLA Modules:
  0.0 376.3 jit_solution(1949500972296927880)
XLA Ops:
  10.8 93.3 %all_to_all.25 = bf16[128,2,4,768]{3,2,1,0:T(4,128)(2,1)S(1)} all-to-all(bf16[128,2,4,768]{3,2,1,0:T(4,128)(2,1)S(1)} %copy.20), channel_id=1, replica_groups=mesh['dp'=4,'expert'=128] {'expert'}, dimensions={0} | all-to-all | bytes 3145728 | tf_op jit(solution)/shard_map/all_to_all | solution.py:26
  107.9 1.5 reshape.46
  109.4 79.7 %all_to_all.26 = bf16[128,2,2816]{2,1,0:T(2,128)(2,1)} all-to-all(bf16[128,2,2816]{2,1,0:T(2,128)(2,1)} %reshape.46), channel_id=1, replica_groups=mesh['dp'=4,'expert'=128] {'expert'}, dimensions={0} | all-to-all | bytes 2883584 | tf_op jit(solution)/shard_map/all_to_all | solution.py:46
  189.2 3.4 reshape.47
  193.8 4.3 %all-to-all-start.3 = ((bf16[4,256,512]{2,1,0:T(8,128)(2,1)}), bf16[4,256,512]{2,1,0:T(8,128)(2,1)}, u32[]{:S(2)}, u32[]{:S(2)}) async-start(bf16[4,256,512]{2,1,0:T(8,128)(2,1)} %pad_maximum_fusion.1), calls=%async_computation.3 | async-start | bytes 2097152 | tf_op jit(solution)/shard_map/all_to_all | solution.py:59
  199.8 1.6 fusion.20
  201.5 1.9 convolution_add_fusion.5
  207.6 1.5 fusion.23
  209.1 1.5 fusion.22
  210.6 1.5 fusion.21
  212.2 1.5 fusion.11
  213.7 1.5 fusion.10
  215.3 1.5 fusion.9
  216.8 1.5 fusion.19
  218.3 1.5 fusion.8
  221.5 10.9 %all-to-all-start.2 = ((bf16[128,2,2048]{2,1,0:T(2,128)(2,1)}), bf16[128,2,2048]{2,1,0:T(2,128)(2,1)S(1)}, u32[]{:S(2)}, u32[]{:S(2)}) async-start(bf16[128,2,2048]{2,1,0:T(2,128)(2,1)} %reshape.48), calls=%async_computation.2 | async-start | bytes 2097152 | tf_op jit(solution)/shard_map/all_to_all | solution.py:91
  232.4 18.1 %all-gather.5.cloned.1.call-done = bf16[1024,1536]{1,0:T(8,128)(2,1)} async-done(((bf16[256,1536]{1,0:T(8,128)(2,1)}), bf16[1024,1536]{1,0:T(8,128)(2,1)}) %all-gather.5.cloned.1.call-update) | async-done | bytes 3145744 | tf_op jit(solution)/shard_map/all_gather | solution.py:74
  250.5 5.2 %convolution_convert_fusion.1 = bf16[512,1536]{1,0:T(8,128)(2,1)} fusion(bf16[1024,512]{1,0:T(8,128)(2,1)} %bitcast.21, bf16[1024,1536]{1,0:T(8,128)(2,1)} %all-gather.5.cloned.1.call-done), kind=kOutput, calls=%fused_computation.1 | convolution fusion | flops 1611399168 | bytes 5767168 | tf_op jit(solution)/shard_map/dot_general | solution.py:99
  255.7 3.6 reshape.51
  259.4 1.8 copy.35
  261.2 23.3 %all-to-all-done.2 = bf16[128,2,2048]{2,1,0:T(2,128)(2,1)S(1)} async-done(((bf16[128,2,2048]{2,1,0:T(2,128)(2,1)}), bf16[128,2,2048]{2,1,0:T(2,128)(2,1)S(1)}, u32[]{:S(2)}, u32[]{:S(2)}) %all-to-all-start.2) | async-done | bytes 1048608 | tf_op jit(solution)/shard_map/all_to_all | solution.py:91
  284.5 10.0 %all-to-all-start.4 = ((bf16[128,2,4,768]{3,2,1,0:T(4,128)(2,1)}), bf16[128,2,4,768]{3,2,1,0:T(4,128)(2,1)S(1)}, u32[]{:S(2)}, u32[]{:S(2)}) async-start(bf16[128,2,4,768]{3,2,1,0:T(4,128)(2,1)} %bitcast.73), calls=%async_computation.4 | async-start | bytes 3145728 | tf_op jit(solution)/shard_map/all_to_all | solution.py:103
  295.7 2.4 convolution_convert_fusion.2
  298.1 69.4 %all-to-all-done.4 = bf16[128,2,4,768]{3,2,1,0:T(4,128)(2,1)S(1)} async-done(((bf16[128,2,4,768]{3,2,1,0:T(4,128)(2,1)}), bf16[128,2,4,768]{3,2,1,0:T(4,128)(2,1)S(1)}, u32[]{:S(2)}, u32[]{:S(2)}) %all-to-all-start.4) | async-done | bytes 1572896 | tf_op jit(solution)/shard_map/all_to_all | solution.py:103
  (44 shorter events, 19.2 us)
Async XLA Ops:
  7.2 1.1 copy-start
  7.2 191.1 %all-gather.3.cloned.1.call-start = ((), (), s32[]{:S(2)}) async-start(), calls=%async_computation.5 | async-start | bytes 7864320 | tf_op jit(solution)/shard_map/all_gather | solution.py:28
  105.4 1.4 copy-start.4
  105.4 1.9 copy-start.3
  105.4 1.9 copy-start.6
  105.4 2.0 copy-start.2
  193.8 27.7 %all-to-all-start.3 = ((bf16[4,256,512]{2,1,0:T(8,128)(2,1)}), bf16[4,256,512]{2,1,0:T(8,128)(2,1)}, u32[]{:S(2)}, u32[]{:S(2)}) async-start(bf16[4,256,512]{2,1,0:T(8,128)(2,1)} %pad_maximum_fusion.1), calls=%async_computation.3 | async-start | bytes 2097152 | tf_op jit(solution)/shard_map/all_to_all | solution.py:59
  198.1 52.5 %all-gather.5.cloned.1.call-start = ((), (), s32[]{:S(2)}) async-start(), calls=%async_computation.6 | async-start | bytes 3932160 | tf_op jit(solution)/shard_map/all_gather | solution.py:74
  199.8 5.1 %copy-start.1 = (bf16[4,2,512,768]{3,2,1,0:T(8,128)(2,1)S(1)}, bf16[4,2,512,768]{3,2,1,0:T(8,128)(2,1)}, u32[]{:S(2)}) copy-start(bf16[4,2,512,768]{3,2,1,0:T(8,128)(2,1)} %all-gather.3.cloned.1.call-done) | copy-start | bytes 18874372
  221.5 62.9 %all-to-all-start.2 = ((bf16[128,2,2048]{2,1,0:T(2,128)(2,1)}), bf16[128,2,2048]{2,1,0:T(2,128)(2,1)S(1)}, u32[]{:S(2)}, u32[]{:S(2)}) async-start(bf16[128,2,2048]{2,1,0:T(2,128)(2,1)} %reshape.48), calls=%async_computation.2 | async-start | bytes 2097152 | tf_op jit(solution)/shard_map/all_to_all | solution.py:91
  284.5 83.0 %all-to-all-start.4 = ((bf16[128,2,4,768]{3,2,1,0:T(4,128)(2,1)}), bf16[128,2,4,768]{3,2,1,0:T(4,128)(2,1)S(1)}, u32[]{:S(2)}, u32[]{:S(2)}) async-start(bf16[128,2,4,768]{3,2,1,0:T(4,128)(2,1)} %bitcast.73), calls=%async_computation.4 | async-start | bytes 3145728 | tf_op jit(solution)/shard_map/all_to_all | solution.py:103
  294.5 73.0 %copy-start.5 = (s32[128]{0:T(128)S(1)}, s32[128]{0:T(128)}, u32[]{:S(2)}) copy-start(s32[128]{0:T(128)} %param.10) | copy-start | bytes 1540
Sparse Core Ops, SparseCore 0:
  106.9 69.4 all-gather.2
  207.7 42.7 all-gather.4

commit v2 on v1

v2 whole, which is shorter than its diff:
```python
import functools

import jax
import jax.numpy as jnp
from jax import lax
from jax.experimental import pallas as pl
from jax.experimental.pallas import tpu as pltpu
from jax.sharding import PartitionSpec as P


def shift(values, distance):
    size = lax.axis_size("dp")
    return lax.ppermute(values, "dp", [(i, (i + distance) % size) for i in range(size)])


def rotate_columns(values, start_block, block):
    doubled = jnp.concatenate([values, values], axis=1)
    return lax.dynamic_slice_in_dim(doubled, start_block * block, values.shape[1], axis=1)


def one_hot(condition):
    return condition.astype(jnp.bfloat16)


def expert_kernel(count, block, hidden, rows_ref, *refs):
    gate_refs, up_refs = refs[:count], refs[count : 2 * count]
    grads_ref, terms_ref = refs[2 * count :]
    gate_sum, up_sum = 0.0, 0.0
    for i in range(count):
        part = rows_ref[:, i * block : (i + 1) * block]
        gate_sum = gate_sum + jnp.dot(part, gate_refs[i][...], preferred_element_type=jnp.float32)
        up_sum = up_sum + jnp.dot(part, up_refs[i][...], preferred_element_type=jnp.float32)
    sigma = 1.0 / (1.0 + jnp.exp(-gate_sum))
    scaled = rows_ref[:, count * block :].astype(jnp.float32)
    grad_gate = (scaled * up_sum * sigma * (1.0 + gate_sum * (1.0 - sigma))).astype(jnp.bfloat16)
    grad_up = (scaled * gate_sum * sigma).astype(jnp.bfloat16)
    grads_ref[:, :hidden] = grad_gate
    grads_ref[:, hidden:] = grad_up
    contract_cols = (((1,), (1,)), ((), ()))
    for i in range(count):
        terms_ref[:, i * block : (i + 1) * block] = (
            lax.dot_general(
                grad_gate, gate_refs[i][...], contract_cols, preferred_element_type=jnp.float32
            )
            + lax.dot_general(
                grad_up, up_refs[i][...], contract_cols, preferred_element_type=jnp.float32
            )
        ).astype(jnp.bfloat16)


def expert_rows(rows, gate_blocks, up_blocks):
    count = len(gate_blocks)
    block, hidden = gate_blocks[0].shape
    depth = rows.shape[0]
    in_vmem = pl.BlockSpec(memory_space=pltpu.VMEM)
    return pl.pallas_call(
        functools.partial(expert_kernel, count, block, hidden),
        out_shape=(
            jax.ShapeDtypeStruct((depth, 2 * hidden), jnp.bfloat16),
            jax.ShapeDtypeStruct((depth, count * block), jnp.bfloat16),
        ),
        in_specs=[in_vmem] * (1 + 2 * count),
        out_specs=(in_vmem, in_vmem),
        compiler_params=pltpu.CompilerParams(vmem_limit_bytes=32 << 20),
        cost_estimate=pl.CostEstimate(
            flops=8 * depth * hidden * count * block,
            bytes_accessed=4 * hidden * count * block + 4 * depth * (count * block + hidden),
            transcendentals=depth * hidden,
        ),
    )(rows, *gate_blocks, *up_blocks)


def per_device(tokens, hidden_grad, gate_prob, slot_choice, replica_plan, weights):
    expert_count = lax.axis_size("expert")
    group_count = lax.axis_size("dp")
    me = lax.axis_index("dp")
    token_count, pick_count = slot_choice.shape
    row_count = token_count * pick_count
    capacity = max(2, 2 * row_count // expert_count)
    depth_rows = expert_count * capacity
    model_width = tokens.shape[1]
    hidden_width = hidden_grad.shape[2]
    expert_total = weights.shape[0]
    shard_rows = weights.shape[2]
    block_rows = shard_rows * expert_count
    routed_width = model_width + hidden_width

    slots = jnp.arange(expert_count, dtype=jnp.int32)
    chooser = one_hot(replica_plan[:, None] == jnp.arange(expert_total, dtype=jnp.int32)[None, :])
    send_weights = jnp.einsum(
        "se,ekdf->skdf", chooser, weights, preferred_element_type=jnp.float32
    ).astype(jnp.bfloat16)
    own = lax.all_to_all(send_weights, "expert", split_axis=0, concat_axis=0, tiled=True)
    own_gate = own[:, 0].reshape(block_rows, hidden_width)
    own_up = own[:, 1].reshape(block_rows, hidden_width)
    left_gate = shift(own_gate, 1)
    right_up = shift(own_up, -1)
    left_up = shift(own_up, 1)
    right_gate = shift(own_gate, -1)
    far_gate = shift(left_gate, 1)
    far_up = shift(right_up, -1)
    gate_blocks = [own_gate, right_gate, far_gate, left_gate]
    up_blocks = [own_up, right_up, far_up, left_up]

    flat_slot = slot_choice.reshape(row_count)
    slot_member = (flat_slot[:, None] == slots[None, :]).astype(jnp.int32)
    ranking = jnp.sum((jnp.cumsum(slot_member, axis=0) - 1) * slot_member, axis=1)
    position = flat_slot * capacity + ranking
    scatter_table = one_hot(jnp.arange(depth_rows, dtype=jnp.int32)[:, None] == position[None, :])
    token_rows = jnp.repeat(rotate_columns(tokens, me, block_rows), pick_count, axis=0)
    cotangent = (gate_prob[:, :, None] * hidden_grad.astype(jnp.float32)).astype(jnp.bfloat16)
    cotangent = cotangent.reshape(row_count, hidden_width)
    routed = jnp.concatenate([token_rows, cotangent], axis=1)
    send_rows = jnp.dot(scatter_table, routed, preferred_element_type=jnp.float32).astype(
        jnp.bfloat16
    )
    send_rows, _ = lax.optimization_barrier(
        (send_rows.reshape(expert_count, capacity, routed_width), own)
    )
    rows = lax.all_to_all(
        send_rows, "expert", split_axis=0, concat_axis=0, tiled=True
    ).reshape(depth_rows, routed_width)

    grads, row_terms = expert_rows(rows, gate_blocks, up_blocks)
    back_rows = lax.all_to_all(
        row_terms.reshape(expert_count, capacity, model_width),
        "expert",
        split_axis=0,
        concat_axis=0,
        tiled=True,
    ).reshape(depth_rows, model_width)

    blocks = [rows[:, i * block_rows : (i + 1) * block_rows] for i in range(group_count)]
    columns = [blocks[0], shift(blocks[3], -1), shift(blocks[2], 2), shift(blocks[1], 1)]
    grads_left = shift(grads, 1)
    grads_right = shift(grads, -1)
    middle = depth_rows // 2
    grads_far = [shift(grads_left[:middle], 1), shift(grads_right[middle:], -1)]
    all_columns = jnp.concatenate(columns, axis=0)
    all_grads = jnp.concatenate([grads, grads_right, *grads_far, grads_left], axis=0)
    contract_rows = (((0,), (0,)), ((), ()))
    summed = lax.dot_general(
        all_columns, all_grads, contract_rows, preferred_element_type=jnp.float32
    ).astype(jnp.bfloat16)
    pieces = summed.reshape(expert_count, shard_rows, 2, hidden_width).transpose(0, 2, 1, 3)
    gathered = lax.all_to_all(pieces, "expert", split_axis=0, concat_axis=0, tiled=True)
    membership = one_hot(
        jnp.arange(expert_total, dtype=jnp.int32)[:, None] == replica_plan[None, :]
    )
    expert_grad = jnp.einsum(
        "es,skdf->ekdf", membership, gathered, preferred_element_type=jnp.float32
    )
    expert_grad = (expert_grad / group_count).astype(jnp.bfloat16)

    token_grads = lax.dot_general(
        scatter_table, back_rows, contract_rows, preferred_element_type=jnp.float32
    )
    input_grad = jnp.sum(token_grads.reshape(token_count, pick_count, model_width), axis=1).astype(
        jnp.bfloat16
    )
    input_grad = rotate_columns(input_grad, (group_count - me) % group_count, block_rows)
    return (input_grad, expert_grad)


def solution(mesh):
    placed = (
        P(("dp", "expert"), None),
        P(("dp", "expert"), None, None),
        P(("dp", "expert"), None),
        P(("dp", "expert"), None),
        P(),
        P(None, None, ("dp", "expert"), None),
    )
    return jax.shard_map(
        per_device,
        mesh=mesh,
        in_specs=placed,
        out_specs=(P(("dp", "expert"), None), P(None, None, ("dp", "expert"), None)),
        check_vma=False,
    )
```

time: 381 us -> 352 us (0.924)
  blocking collectives: 173 us -> 0 us
  waiting for transfers between devices: 111 us -> 202 us
  starting transfers between devices: 25.4 us -> 102 us
  matrix products: 30.3 us -> 6.73 us
  between operations: 14.4 us -> 1.1 us
  local copies, waits for them, and re-layouts: 19.6 us -> 27.7 us
  Pallas kernels: 0 us -> 6.12 us
    all_to_all x2 -> x0, blocking collectives: 173 us -> none  [the longest x1 93.3 us: per_device(): lax.all_to_all(send_weights, 'expert', split_axis=0, concat_axis=0, tiled...]
    all_to_all x1 -> x2, waiting for transfers between devices: 0.01 us -> 102 us  [the longest x1 66.2 us: per_device(): lax.all_to_all(send_weights, 'expert', split_axis=0, concat_axis=0, tiled...]
    ppermute x0 -> x13, starting transfers between devices: none -> 40.7 us  [shift(): lax.ppermute(values, 'dp', [(i, (i + distance) % size) for i in range(siz...]
    ppermute x0 -> x13, waiting for transfers between devices: none -> 29.5 us  [shift(): lax.ppermute(values, 'dp', [(i, (i + distance) % size) for i in range(siz...]
    all_to_all x1 -> x2, starting transfers between devices: 4.26 us -> 32.7 us  [the longest x1 20.7 us: per_device(): lax.all_to_all(send_weights, 'expert', split_axis=0, concat_axis=0, tiled...]
    dot_general x18 -> x2, matrix products: 28 us -> 3.32 us  [the longest x1 2.97 us: per_device(): lax.dot_general(all_columns, all_grads, contract_rows, preferred_element_...]
    all_to_all x1, waiting for transfers between devices: 23.3 us -> 0.54 us  [per_device(): lax.all_to_all(row_terms.reshape(expert_count, capacity, model_width), 'e...]
    all_gather x2 -> x0, waiting for transfers between devices: 18.2 us -> none  [the longest x1 18.1 us: per_device(): all_grads = lax.all_gather(grads, 'dp', axis=0, tiled=True)]
  transfers between devices with their start and end apart: 5 -> 17, of which waited for: 3 -> 9; matrix products, arithmetic and copies ran while one was open for 12% -> 8% of each run, Pallas kernels for 0% -> 0%
where the time goes in v2:
time: 352 us; the launch traced here: 347 us
  waiting for transfers between devices  202 us (57%)
  starting transfers between devices  102 us (29%)
  local copies, waits for them, and re-layouts  27.7 us (8%)
  matrix products  6.73 us (2%)
  Pallas kernels  6.12 us (2%)
    all_to_all x1, waiting for transfers between devices, per_device(): lax.all_to_all(pieces, 'expert', split_axis=0, concat_axis=0, tiled=True)  70 us
    all_to_all x1, waiting for transfers between devices, per_device(): lax.all_to_all(send_weights, 'expert', split_axis=0, concat_axis=0, tiled...  66.2 us
    ppermute x13, starting transfers between devices, shift(): lax.ppermute(values, 'dp', [(i, (i + distance) % size) for i in range(siz...  40.7 us
    all_to_all x1, waiting for transfers between devices, per_device(): lax.all_to_all(send_rows, 'expert', split_axis=0, concat_axis=0, tiled=True)  35.4 us
    ppermute x13, waiting for transfers between devices, shift(): lax.ppermute(values, 'dp', [(i, (i + distance) % size) for i in range(siz...  29.5 us
    all_to_all x1, starting transfers between devices, per_device(): lax.all_to_all(send_weights, 'expert', split_axis=0, concat_axis=0, tiled...  20.7 us
    all_to_all x1, starting transfers between devices, per_device(): lax.all_to_all(pieces, 'expert', split_axis=0, concat_axis=0, tiled=True)  17.2 us
    all_to_all x1, starting transfers between devices, per_device(): lax.all_to_all(send_rows, 'expert', split_axis=0, concat_axis=0, tiled=True)  12 us
  transfers between devices with their start and end apart: 17, of which 9 were waited for; matrix products, arithmetic and copies ran while one was open for 8% of the time, Pallas kernels for 0%

profile of v2, /device:TPU:1, one launch (start us, length us, event | category | flops | bytes accessed | tf_op | source)
XLA Modules:
  0.0 347.3 jit_solution(16292789673727423989)
XLA Ops:
  5.4 20.7 %all-to-all-start = ((bf16[128,2,4,768]{3,2,1,0:T(4,128)(2,1)}), bf16[128,2,4,768]{3,2,1,0:T(4,128)(2,1)S(1)}, u32[]{:S(2)}, u32[]{:S(2)}) async-start(bf16[128,2,4,768]{3,2,1,0:T(4,128)(2,1)} %copy.14), calls=%async_computation | async-start | bytes 3145728 | tf_op jit(solution)/shard_map/all_to_all | solution.py:93
  28.6 4.2 %reshape.43 = bf16[128,2,2816]{2,1,0:T(2,128)(2,1)} reshape(bf16[256,2816]{1,0:T(8,128)(2,1)} %convolution_convert_fusion) | data formatting | bytes 2883584 | tf_op jit(solution)/shard_map/reshape | solution.py:118
  32.8 66.2 %all-to-all-done = bf16[128,2,4,768]{3,2,1,0:T(4,128)(2,1)S(1)} async-done(((bf16[128,2,4,768]{3,2,1,0:T(4,128)(2,1)}), bf16[128,2,4,768]{3,2,1,0:T(4,128)(2,1)S(1)}, u32[]{:S(2)}, u32[]{:S(2)}) %all-to-all-start) | async-done | bytes 1572896 | tf_op jit(solution)/shard_map/all_to_all | solution.py:93
  99.1 12.0 %all-to-all-start.1 = ((bf16[128,2,2816]{2,1,0:T(2,128)(2,1)}), bf16[128,2,2816]{2,1,0:T(2,128)(2,1)}, u32[]{:S(2)}, u32[]{:S(2)}) async-start(bf16[128,2,2816]{2,1,0:T(2,128)(2,1)} %reshape.43), calls=%async_computation.1 | async-start | bytes 2883584 | tf_op jit(solution)/shard_map/all_to_all | solution.py:120
  114.4 3.1 collective-permute-start.1
  118.6 3.4 collective-permute-start.3
  122.0 3.2 collective-permute-start
  127.3 8.5 %collective-permute-done.1.refs_3_ = bf16[512,768]{1,0:T(8,128)(2,1)} collective-permute-done((bf16[512,768]{1,0:T(8,128)(2,1)S(1)}, bf16[512,768]{1,0:T(8,128)(2,1)}, u32[]{:S(2)}, u32[]{:S(2)}) %collective-permute-start.1) | collective-permute-done | bytes 786464 | tf_op jit(solution)/shard_map/ppermute | solution.py:13
  138.7 4.8 %collective-permute-start.4 = (bf16[512,768]{1,0:T(8,128)(2,1)}, bf16[512,768]{1,0:T(8,128)(2,1)}, u32[]{:S(2)}, u32[]{:S(2)}) collective-permute-start(bf16[512,768]{1,0:T(8,128)(2,1)} %collective-permute-done.3.refs_5_), channel_id=1, source_target_pairs={{0,384},{128,0},{256,128},{384,256},{1,385},{129,1},{257,129},{385... | collective-permute-start | bytes 2359304 | tf_op jit(solution)/shard_map/ppermute | solution.py:13
  143.5 35.4 %all-to-all-done.1 = bf16[128,2,2816]{2,1,0:T(2,128)(2,1)} async-done(((bf16[128,2,2816]{2,1,0:T(2,128)(2,1)}), bf16[128,2,2816]{2,1,0:T(2,128)(2,1)}, u32[]{:S(2)}, u32[]{:S(2)}) %all-to-all-start.1) | async-done | bytes 1441824 | tf_op jit(solution)/shard_map/all_to_all | solution.py:120
  178.8 3.4 reshape.44.rows_ref
  183.4 6.1 %shard_map.77 = (bf16[256,1536]{1,0:T(8,128)(2,1)S(1)}, bf16[256,2048]{1,0:T(8,128)(2,1)S(1)}) custom-call(bf16[256,2816]{1,0:T(8,128)(2,1)S(1)} %reshape.44.rows_ref, bf16[512,768]{1,0:T(8,128)(2,1)S(1)} %copy-done.2, bf16[512,768]{1,0:T(8,128)(2,1)} %collective-permute-done.refs_1_, bf16[512,768]{1,0:T(8,128)(2,1)} %collective-permute-done.2.refs_2_, ...), custom_call_target="tpu_custom_call" | custom-call | flops 3221225472 | bytes 9175040 | tf_op jit(solution)/shard_map/pallas_call | solution.py:56
  191.9 11.4 %all-to-all-start.2 = ((bf16[128,2,2048]{2,1,0:T(2,128)(2,1)}), bf16[128,2,2048]{2,1,0:T(2,128)(2,1)}, u32[]{:S(2)}, u32[]{:S(2)}) async-start(bf16[128,2,2048]{2,1,0:T(2,128)(2,1)} %reshape.45), calls=%async_computation.2 | async-start | bytes 2097152 | tf_op jit(solution)/shard_map/all_to_all | solution.py:125
  203.4 3.1 collective-permute-start.10
  206.5 3.4 collective-permute-start.9
  211.9 4.3 %collective-permute-start.7 = (bf16[256,512]{1,0:T(8,128)(2,1)S(1)}, bf16[256,512]{1,0:T(8,128)(2,1)S(1)}, u32[]{:S(2)}, u32[]{:S(2)}) collective-permute-start(bf16[256,512]{1,0:T(8,128)(2,1)S(1)} %get-tuple-element.16), channel_id=1, source_target_pairs={{0,256},{128,384},{256,0},{384,128},{1,257},{129,385},{257,1},{385... | collective-permute-start | bytes 786440 | tf_op jit(solution)/shard_map/ppermute | solution.py:13
  216.3 3.1 collective-permute-start.6
  219.3 5.4 %collective-permute-done.10 = bf16[256,1536]{1,0:T(8,128)(2,1)S(1)} collective-permute-done((bf16[256,1536]{1,0:T(8,128)(2,1)S(1)}, bf16[256,1536]{1,0:T(8,128)(2,1)S(1)}, u32[]{:S(2)}, u32[]{:S(2)}) %collective-permute-start.10) | collective-permute-done | bytes 786464 | tf_op jit(solution)/shard_map/ppermute | solution.py:13
  226.8 4.6 %collective-permute-start.12 = (bf16[128,1536]{1,0:T(8,128)(2,1)S(1)}, bf16[128,1536]{1,0:T(8,128)(2,1)S(1)}, u32[]{:S(2)}, u32[]{:S(2)}) collective-permute-start(bf16[128,1536]{1,0:T(8,128)(2,1)S(1)} %slice.39), channel_id=1, source_target_pairs={{0,384},{128,0},{256,128},{384,256},{1,385},{129,1},{257,129},{385... | collective-permute-start | bytes 1179656 | tf_op jit(solution)/shard_map/ppermute | solution.py:13
  231.4 13.3 %collective-permute-done.11 = bf16[128,1536]{1,0:T(8,128)(2,1)S(1)} collective-permute-done((bf16[128,1536]{1,0:T(8,128)(2,1)S(1)}, bf16[128,1536]{1,0:T(8,128)(2,1)S(1)}, u32[]{:S(2)}, u32[]{:S(2)}) %collective-permute-start.11) | collective-permute-done | bytes 393248 | tf_op jit(solution)/shard_map/ppermute | solution.py:13
  246.2 3.0 convolution_convert_fusion.1
  249.1 3.6 %reshape.47 = bf16[128,4,2,768]{3,2,1,0:T(2,128)(2,1)S(1)} reshape(bf16[512,1536]{1,0:T(8,128)(2,1)} %convolution_convert_fusion.1) | data formatting | bytes 3145728 | tf_op jit(solution)/shard_map/reshape | solution.py:145
  255.1 17.2 %all-to-all-start.3 = ((bf16[128,2,4,768]{3,2,1,0:T(4,128)(2,1)}), bf16[128,2,4,768]{3,2,1,0:T(4,128)(2,1)S(1)}, u32[]{:S(2)}, u32[]{:S(2)}) async-start(bf16[128,2,4,768]{3,2,1,0:T(4,128)(2,1)} %bitcast.19), calls=%async_computation.3 | async-start | bytes 3145728 | tf_op jit(solution)/shard_map/all_to_all | solution.py:146
  275.2 70.0 %all-to-all-done.3 = bf16[128,2,4,768]{3,2,1,0:T(4,128)(2,1)S(1)} async-done(((bf16[128,2,4,768]{3,2,1,0:T(4,128)(2,1)}), bf16[128,2,4,768]{3,2,1,0:T(4,128)(2,1)S(1)}, u32[]{:S(2)}, u32[]{:S(2)}) %all-to-all-start.3) | async-done | bytes 1572896 | tf_op jit(solution)/shard_map/all_to_all | solution.py:146
  (64 shorter events, 32.9 us)
Async XLA Ops:
  5.4 20.7 %copy-start.8 = (s32[128,1]{0,1:T(1,128)S(1)}, s32[128,1]{0,1:T(1,128)}, u32[]{:S(2)}) copy-start(s32[128,1]{0,1:T(1,128)} %param.9) | copy-start | bytes 1540
  5.4 21.2 %copy-start.7 = (bf16[128,1,768]{2,0,1:T(8,128)(2,1)S(1)}, bf16[128,1,768]{2,0,1:T(8,128)(2,1)}, u32[]{:S(2)}) copy-start(bf16[128,1,768]{2,0,1:T(8,128)(2,1)} %param.7) | copy-start | bytes 589828
  5.4 21.2 %copy-start.10 = (f32[128,1]{0,1:T(1,128)S(1)}, f32[128,1]{0,1:T(1,128)}, u32[]{:S(2)}) copy-start(f32[128,1]{0,1:T(1,128)} %param.8) | copy-start | bytes 1540
  5.4 21.3 %copy-start.6 = (bf16[128,2048]{1,0:T(8,128)(2,1)S(1)}, bf16[128,2048]{1,0:T(8,128)(2,1)}, u32[]{:S(2)}) copy-start(bf16[128,2048]{1,0:T(8,128)(2,1)} %param.6) | copy-start | bytes 1572868
  5.4 93.7 %all-to-all-start = ((bf16[128,2,4,768]{3,2,1,0:T(4,128)(2,1)}), bf16[128,2,4,768]{3,2,1,0:T(4,128)(2,1)S(1)}, u32[]{:S(2)}, u32[]{:S(2)}) async-start(bf16[128,2,4,768]{3,2,1,0:T(4,128)(2,1)} %copy.14), calls=%async_computation | async-start | bytes 3145728 | tf_op jit(solution)/shard_map/all_to_all | solution.py:93
  99.1 79.7 %all-to-all-start.1 = ((bf16[128,2,2816]{2,1,0:T(2,128)(2,1)}), bf16[128,2,2816]{2,1,0:T(2,128)(2,1)}, u32[]{:S(2)}, u32[]{:S(2)}) async-start(bf16[128,2,2816]{2,1,0:T(2,128)(2,1)} %reshape.43), calls=%async_computation.1 | async-start | bytes 2883584 | tf_op jit(solution)/shard_map/all_to_all | solution.py:120
  114.4 67.8 %copy-start.1 = (bf16[512,768]{1,0:T(8,128)(2,1)}, bf16[512,768]{1,0:T(8,128)(2,1)S(1)}, u32[]{:S(2)}) copy-start(bf16[512,768]{1,0:T(8,128)(2,1)S(1)} %reshape_squeeze.6.refs_0_) | copy-start | bytes 2359300
  114.4 21.4 %collective-permute-start.1 = (bf16[512,768]{1,0:T(8,128)(2,1)S(1)}, bf16[512,768]{1,0:T(8,128)(2,1)}, u32[]{:S(2)}, u32[]{:S(2)}) collective-permute-start(bf16[512,768]{1,0:T(8,128)(2,1)S(1)} %reshape_squeeze.6.refs_0_), channel_id=1, source_target_pairs={{0,128},{128,256},{256,384},{384,0},{1,129},{129,257},{257,385},{3... | collective-permute-start | bytes 2359304 | tf_op jit(solution)/shard_map/ppermute | solution.py:13
  118.6 20.1 %collective-permute-start.3 = (bf16[512,768]{1,0:T(8,128)(2,1)}, bf16[512,768]{1,0:T(8,128)(2,1)}, u32[]{:S(2)}, u32[]{:S(2)}) collective-permute-start(bf16[512,768]{1,0:T(8,128)(2,1)} %reshape_squeeze.7.refs_4_), channel_id=1, source_target_pairs={{0,384},{128,0},{256,128},{384,256},{1,385},{129,1},{257,129},{385... | collective-permute-start | bytes 2359304 | tf_op jit(solution)/shard_map/ppermute | solution.py:13
  122.0 60.2 %collective-permute-start = (bf16[512,768]{1,0:T(8,128)(2,1)S(1)}, bf16[512,768]{1,0:T(8,128)(2,1)}, u32[]{:S(2)}, u32[]{:S(2)}) collective-permute-start(bf16[512,768]{1,0:T(8,128)(2,1)S(1)} %reshape_squeeze.6.refs_0_), channel_id=1, source_target_pairs={{0,384},{128,0},{256,128},{384,256},{1,385},{129,1},{257,129},{385... | collective-permute-start | bytes 2359304 | tf_op jit(solution)/shard_map/ppermute | solution.py:13
  125.2 57.1 %collective-permute-start.5 = (bf16[512,768]{1,0:T(8,128)(2,1)}, bf16[512,768]{1,0:T(8,128)(2,1)}, u32[]{:S(2)}, u32[]{:S(2)}) collective-permute-start(bf16[512,768]{1,0:T(8,128)(2,1)} %reshape_squeeze.7.refs_4_), channel_id=1, source_target_pairs={{0,128},{128,256},{256,384},{384,0},{1,129},{129,257},{257,385},{3... | collective-permute-start | bytes 2359304 | tf_op jit(solution)/shard_map/ppermute | solution.py:13
  135.8 46.5 %collective-permute-start.2 = (bf16[512,768]{1,0:T(8,128)(2,1)}, bf16[512,768]{1,0:T(8,128)(2,1)}, u32[]{:S(2)}, u32[]{:S(2)}) collective-permute-start(bf16[512,768]{1,0:T(8,128)(2,1)} %collective-permute-done.1.refs_3_), channel_id=1, source_target_pairs={{0,128},{128,256},{256,384},{384,0},{1,129},{129,257},{257,385},{3... | collective-permute-start | bytes 2359304 | tf_op jit(solution)/shard_map/ppermute | solution.py:13
  138.7 43.6 %collective-permute-start.4 = (bf16[512,768]{1,0:T(8,128)(2,1)}, bf16[512,768]{1,0:T(8,128)(2,1)}, u32[]{:S(2)}, u32[]{:S(2)}) collective-permute-start(bf16[512,768]{1,0:T(8,128)(2,1)} %collective-permute-done.3.refs_5_), channel_id=1, source_target_pairs={{0,384},{128,0},{256,128},{384,256},{1,385},{129,1},{257,129},{385... | collective-permute-start | bytes 2359304 | tf_op jit(solution)/shard_map/ppermute | solution.py:13
  191.9 11.4 %copy-start.4 = (bf16[256,1536]{1,0:T(8,128)(2,1)S(1)}, bf16[256,1536]{1,0:T(8,128)(2,1)}, u32[]{:S(2)}) copy-start(bf16[256,1536]{1,0:T(8,128)(2,1)} %copy-done.3) | copy-start | bytes 2359300
  191.9 63.2 %all-to-all-start.2 = ((bf16[128,2,2048]{2,1,0:T(2,128)(2,1)}), bf16[128,2,2048]{2,1,0:T(2,128)(2,1)}, u32[]{:S(2)}, u32[]{:S(2)}) async-start(bf16[128,2,2048]{2,1,0:T(2,128)(2,1)} %reshape.45), calls=%async_computation.2 | async-start | bytes 2097152 | tf_op jit(solution)/shard_map/all_to_all | solution.py:125
  203.4 21.3 %collective-permute-start.10 = (bf16[256,1536]{1,0:T(8,128)(2,1)S(1)}, bf16[256,1536]{1,0:T(8,128)(2,1)S(1)}, u32[]{:S(2)}, u32[]{:S(2)}) collective-permute-start(bf16[256,1536]{1,0:T(8,128)(2,1)S(1)} %copy-done.4), channel_id=1, source_target_pairs={{0,128},{128,256},{256,384},{384,0},{1,129},{129,257},{257,385},{3... | collective-permute-start | bytes 2359304 | tf_op jit(solution)/shard_map/ppermute | solution.py:13
  206.5 20.2 %collective-permute-start.9 = (bf16[256,1536]{1,0:T(8,128)(2,1)S(1)}, bf16[256,1536]{1,0:T(8,128)(2,1)S(1)}, u32[]{:S(2)}, u32[]{:S(2)}) collective-permute-start(bf16[256,1536]{1,0:T(8,128)(2,1)S(1)} %copy-done.4), channel_id=1, source_target_pairs={{0,384},{128,0},{256,128},{384,256},{1,385},{129,1},{257,129},{385... | collective-permute-start | bytes 2359304 | tf_op jit(solution)/shard_map/ppermute | solution.py:13
  210.0 36.2 %collective-permute-start.8 = (bf16[256,512]{1,0:T(8,128)(2,1)S(1)}, bf16[256,512]{1,0:T(8,128)(2,1)S(1)}, u32[]{:S(2)}, u32[]{:S(2)}) collective-permute-start(bf16[256,512]{1,0:T(8,128)(2,1)S(1)} %get-tuple-element.15), channel_id=1, source_target_pairs={{0,128},{128,256},{256,384},{384,0},{1,129},{129,257},{257,385},{3... | collective-permute-start | bytes 786440 | tf_op jit(solution)/shard_map/ppermute | solution.py:13
  211.9 34.3 %collective-permute-start.7 = (bf16[256,512]{1,0:T(8,128)(2,1)S(1)}, bf16[256,512]{1,0:T(8,128)(2,1)S(1)}, u32[]{:S(2)}, u32[]{:S(2)}) collective-permute-start(bf16[256,512]{1,0:T(8,128)(2,1)S(1)} %get-tuple-element.16), channel_id=1, source_target_pairs={{0,256},{128,384},{256,0},{384,128},{1,257},{129,385},{257,1},{385... | collective-permute-start | bytes 786440 | tf_op jit(solution)/shard_map/ppermute | solution.py:13
  216.3 29.9 %collective-permute-start.6 = (bf16[256,512]{1,0:T(8,128)(2,1)S(1)}, bf16[256,512]{1,0:T(8,128)(2,1)S(1)}, u32[]{:S(2)}, u32[]{:S(2)}) collective-permute-start(bf16[256,512]{1,0:T(8,128)(2,1)S(1)} %get-tuple-element.17), channel_id=1, source_target_pairs={{0,384},{128,0},{256,128},{384,256},{1,385},{129,1},{257,129},{385... | collective-permute-start | bytes 786440 | tf_op jit(solution)/shard_map/ppermute | solution.py:13
  224.7 20.0 %collective-permute-start.11 = (bf16[128,1536]{1,0:T(8,128)(2,1)S(1)}, bf16[128,1536]{1,0:T(8,128)(2,1)S(1)}, u32[]{:S(2)}, u32[]{:S(2)}) collective-permute-start(bf16[128,1536]{1,0:T(8,128)(2,1)S(1)} %slice.38), channel_id=1, source_target_pairs={{0,128},{128,256},{256,384},{384,0},{1,129},{129,257},{257,385},{3... | collective-permute-start | bytes 1179656 | tf_op jit(solution)/shard_map/ppermute | solution.py:13
  226.8 19.3 %collective-permute-start.12 = (bf16[128,1536]{1,0:T(8,128)(2,1)S(1)}, bf16[128,1536]{1,0:T(8,128)(2,1)S(1)}, u32[]{:S(2)}, u32[]{:S(2)}) collective-permute-start(bf16[128,1536]{1,0:T(8,128)(2,1)S(1)} %slice.39), channel_id=1, source_target_pairs={{0,384},{128,0},{256,128},{384,256},{1,385},{129,1},{257,129},{385... | collective-permute-start | bytes 1179656 | tf_op jit(solution)/shard_map/ppermute | solution.py:13
  255.1 90.2 %all-to-all-start.3 = ((bf16[128,2,4,768]{3,2,1,0:T(4,128)(2,1)}), bf16[128,2,4,768]{3,2,1,0:T(4,128)(2,1)S(1)}, u32[]{:S(2)}, u32[]{:S(2)}) async-start(bf16[128,2,4,768]{3,2,1,0:T(4,128)(2,1)} %bitcast.19), calls=%async_computation.3 | async-start | bytes 3145728 | tf_op jit(solution)/shard_map/all_to_all | solution.py:146
  272.3 73.0 %copy-start.9 = (s32[128]{0:T(128)S(1)}, s32[128]{0:T(128)}, u32[]{:S(2)}) copy-start(s32[128]{0:T(128)} %param.10) | copy-start | bytes 1540
  (4 other events, 7.9 us)

commit v3 on v2

--- a/solution.py
+++ b/solution.py
@@ -70,6 +70,109 @@
     )(rows, *gate_blocks, *up_blocks)
 
 
+PLANE = 8
+
+
+def exchange_kernel(
+    total, send_ref, recv_ref, relay_ref, self_sem, send_sem, recv_sem, out_sem, in_sem, pass_sem
+):
+    me = lax.axis_index("expert")
+    planes, half = total // PLANE, PLANE // 2
+    plane, seat = me // PLANE, me % PLANE
+
+    def device(step, place):
+        return ((plane + step + planes) % planes) * PLANE + place
+
+    def send(target):
+        pltpu.make_async_remote_copy(
+            src_ref=send_ref.at[target],
+            dst_ref=recv_ref.at[me],
+            send_sem=send_sem,
+            recv_sem=recv_sem,
+            device_id={"expert": target},
+            device_id_type=pl.DeviceIdType.MESH,
+        ).start()
+
+    barrier = pltpu.get_barrier_semaphore()
+
+    def greet(step, carry):
+        pl.semaphore_signal(
+            barrier,
+            inc=1,
+            device_id={"expert": (me + step) % total},
+            device_id_type=pl.DeviceIdType.MESH,
+        )
+        return carry
+
+    lax.fori_loop(1, total, greet, 0)
+    pl.semaphore_wait(barrier, total - 1)
+
+    relay = pltpu.make_async_remote_copy(
+        src_ref=send_ref.at[pl.ds(device(planes // 2, half), half)],
+        dst_ref=relay_ref,
+        send_sem=out_sem,
+        recv_sem=in_sem,
+        device_id={"expert": device(-(planes // 4), seat)},
+        device_id_type=pl.DeviceIdType.MESH,
+    )
+    relay.start()
+    for place in range(half):
+        send(device(planes // 2, place))
+    own = pltpu.make_async_copy(send_ref.at[me], recv_ref.at[me], self_sem)
+    own.start()
+
+    def both_ways(item, carry):
+        step = planes // 2 - 1 - item // PLANE
+        place = (seat + item) % PLANE
+        send(device(step, place))
+        send(device(-step, place))
+        return carry
+
+    def same_plane(step, carry):
+        send(device(0, (seat + step) % PLANE))
+        return carry
+
+    pairs = (planes // 2 - 1) * PLANE
+    lax.fori_loop(0, pairs // 2, both_ways, 0)
+    relay.wait_recv()
+    source = device(planes // 4, seat)
+    for place in range(half):
+        pltpu.make_async_remote_copy(
+            src_ref=relay_ref.at[place],
+            dst_ref=recv_ref.at[source],
+            send_sem=pass_sem,
+            recv_sem=recv_sem,
+            device_id={"expert": device(-(planes // 4), half + place)},
+            device_id_type=pl.DeviceIdType.MESH,
+        ).start()
+    lax.fori_loop(pairs // 2, pairs, both_ways, 0)
+    lax.fori_loop(1, PLANE, same_plane, 0)
+
+    own.wait()
+    relay.wait_send()
+    pltpu.make_async_copy(relay_ref, relay_ref, pass_sem).wait()
+    sent = send_ref.at[pl.ds(0, total - 1 - half)]
+    pltpu.make_async_copy(sent, sent, send_sem).wait()
+    landed = recv_ref.at[pl.ds(0, total - 1)]
+    pltpu.make_async_copy(landed, landed, recv_sem).wait()
+
+
+def exchange(pieces):
+    total = pieces.shape[0]
+    in_place = pl.BlockSpec(memory_space=pl.ANY)
+    return pl.pallas_call(
+        functools.partial(exchange_kernel, total),
+        out_shape=jax.ShapeDtypeStruct(pieces.shape, pieces.dtype),
+        in_specs=[in_place],
+        out_specs=in_place,
+        scratch_shapes=[pltpu.VMEM((PLANE // 2, *pieces.shape[1:]), pieces.dtype)]
+        + [pltpu.SemaphoreType.DMA] * 6,
+        compiler_params=pltpu.CompilerParams(
+            collective_id=0, has_side_effects=True, vmem_limit_bytes=4 << 20
+        ),
+    )(pieces)
+
+
 def per_device(tokens, hidden_grad, gate_prob, slot_choice, replica_plan, weights):
     expert_count = lax.axis_size("expert")
     group_count = lax.axis_size("dp")
@@ -143,7 +246,7 @@
         all_columns, all_grads, contract_rows, preferred_element_type=jnp.float32
     ).astype(jnp.bfloat16)
     pieces = summed.reshape(expert_count, shard_rows, 2, hidden_width).transpose(0, 2, 1, 3)
-    gathered = lax.all_to_all(pieces, "expert", split_axis=0, concat_axis=0, tiled=True)
+    gathered = exchange(pieces)
     membership = one_hot(
         jnp.arange(expert_total, dtype=jnp.int32)[:, None] == replica_plan[None, :]
     )

time: 352 us -> 351 us (level)
  Pallas kernels: 6.12 us -> 96.2 us
  waiting for transfers between devices: 202 us -> 128 us
  starting transfers between devices: 102 us -> 85.1 us
    pallas_call x0 -> x1, Pallas kernels: none -> 90.1 us  [exchange(): pl.pallas_call(functools.partial(exchange_kernel, total), out_shape=jax.S...]
    all_to_all x1 -> x0, waiting for transfers between devices: 70 us -> none  [per_device(): lax.all_to_all(pieces, 'expert', split_axis=0, concat_axis=0, tiled=True)]
    all_to_all x1 -> x0, starting transfers between devices: 17.2 us -> none  [per_device(): lax.all_to_all(pieces, 'expert', split_axis=0, concat_axis=0, tiled=True)]
  transfers between devices with their start and end apart: 17 -> 16, of which waited for: 9 -> 7; matrix products, arithmetic and copies ran while one was open for 8% -> 8% of each run, Pallas kernels for 0% -> 26%
where the time goes in v3:
time: 351 us; the launch traced here: 350 us
  waiting for transfers between devices  128 us (36%)
  Pallas kernels  96.2 us (27%)
  starting transfers between devices  85.1 us (24%)
  local copies, waits for them, and re-layouts  30.8 us (9%)
  matrix products  6.72 us (2%)
    pallas_call x1, Pallas kernels, exchange(): pl.pallas_call(functools.partial(exchange_kernel, total), out_shape=jax.S...  90.1 us
    all_to_all x1, waiting for transfers between devices, per_device(): lax.all_to_all(send_weights, 'expert', split_axis=0, concat_axis=0, tiled...  66.2 us
    ppermute x13, starting transfers between devices, shift(): lax.ppermute(values, 'dp', [(i, (i + distance) % size) for i in range(siz...  41 us
    all_to_all x1, waiting for transfers between devices, per_device(): lax.all_to_all(send_rows, 'expert', split_axis=0, concat_axis=0, tiled=True)  35.4 us
    ppermute x13, waiting for transfers between devices, shift(): lax.ppermute(values, 'dp', [(i, (i + distance) % size) for i in range(siz...  26.1 us
    all_to_all x1, starting transfers between devices, per_device(): lax.all_to_all(send_weights, 'expert', split_axis=0, concat_axis=0, tiled...  20.7 us
    all_to_all x1, starting transfers between devices, per_device(): lax.all_to_all(send_rows, 'expert', split_axis=0, concat_axis=0, tiled=True)  12 us
    all_to_all x1, starting transfers between devices, per_device(): lax.all_to_all(row_terms.reshape(expert_count, capacity, model_width), 'e...  11.4 us
  transfers between devices with their start and end apart: 16, of which 7 were waited for; matrix products, arithmetic and copies ran while one was open for 8% of the time, Pallas kernels for 26%

profile of v3, /device:TPU:1, one launch (start us, length us, event | category | flops | bytes accessed | tf_op | source)
XLA Modules:
  0.0 349.6 jit_solution(2208447709565330348)
XLA Ops:
  3.0 2.3 copy.20
  5.4 20.7 %all-to-all-start = ((bf16[128,2,4,768]{3,2,1,0:T(4,128)(2,1)}), bf16[128,2,4,768]{3,2,1,0:T(4,128)(2,1)S(1)}, u32[]{:S(2)}, u32[]{:S(2)}) async-start(bf16[128,2,4,768]{3,2,1,0:T(4,128)(2,1)} %copy.20), calls=%async_computation | async-start | bytes 3145728 | tf_op jit(solution)/shard_map/all_to_all | solution.py:196
  28.6 4.2 %reshape.43 = bf16[128,2,2816]{2,1,0:T(2,128)(2,1)} reshape(bf16[256,2816]{1,0:T(8,128)(2,1)} %convolution_convert_fusion) | data formatting | bytes 2883584 | tf_op jit(solution)/shard_map/reshape | solution.py:221
  32.8 66.2 %all-to-all-done = bf16[128,2,4,768]{3,2,1,0:T(4,128)(2,1)S(1)} async-done(((bf16[128,2,4,768]{3,2,1,0:T(4,128)(2,1)}), bf16[128,2,4,768]{3,2,1,0:T(4,128)(2,1)S(1)}, u32[]{:S(2)}, u32[]{:S(2)}) %all-to-all-start) | async-done | bytes 1572896 | tf_op jit(solution)/shard_map/all_to_all | solution.py:196
  99.1 12.0 %all-to-all-start.1 = ((bf16[128,2,2816]{2,1,0:T(2,128)(2,1)}), bf16[128,2,2816]{2,1,0:T(2,128)(2,1)}, u32[]{:S(2)}, u32[]{:S(2)}) async-start(bf16[128,2,2816]{2,1,0:T(2,128)(2,1)} %reshape.43), calls=%async_computation.1 | async-start | bytes 2883584 | tf_op jit(solution)/shard_map/all_to_all | solution.py:223
  114.4 3.1 collective-permute-start.1
  118.6 3.4 collective-permute-start.3
  122.0 3.2 collective-permute-start
  127.3 8.5 %collective-permute-done.1.refs_3_ = bf16[512,768]{1,0:T(8,128)(2,1)} collective-permute-done((bf16[512,768]{1,0:T(8,128)(2,1)S(1)}, bf16[512,768]{1,0:T(8,128)(2,1)}, u32[]{:S(2)}, u32[]{:S(2)}) %collective-permute-start.1) | collective-permute-done | bytes 786464 | tf_op jit(solution)/shard_map/ppermute | solution.py:13
  138.7 4.8 %collective-permute-start.4 = (bf16[512,768]{1,0:T(8,128)(2,1)}, bf16[512,768]{1,0:T(8,128)(2,1)}, u32[]{:S(2)}, u32[]{:S(2)}) collective-permute-start(bf16[512,768]{1,0:T(8,128)(2,1)} %collective-permute-done.3.refs_5_), channel_id=1, source_target_pairs={{0,384},{128,0},{256,128},{384,256},{1,385},{129,1},{257,129},{385... | collective-permute-start | bytes 2359304 | tf_op jit(solution)/shard_map/ppermute | solution.py:13
  143.5 35.4 %all-to-all-done.1 = bf16[128,2,2816]{2,1,0:T(2,128)(2,1)} async-done(((bf16[128,2,2816]{2,1,0:T(2,128)(2,1)}), bf16[128,2,2816]{2,1,0:T(2,128)(2,1)}, u32[]{:S(2)}, u32[]{:S(2)}) %all-to-all-start.1) | async-done | bytes 1441824 | tf_op jit(solution)/shard_map/all_to_all | solution.py:223
  178.8 3.4 reshape.44.rows_ref
  183.4 6.1 %shard_map.77 = (bf16[256,1536]{1,0:T(8,128)(2,1)S(1)}, bf16[256,2048]{1,0:T(8,128)(2,1)S(1)}) custom-call(bf16[256,2816]{1,0:T(8,128)(2,1)S(1)} %reshape.44.rows_ref, bf16[512,768]{1,0:T(8,128)(2,1)S(1)} %copy-done.4, bf16[512,768]{1,0:T(8,128)(2,1)} %collective-permute-done.refs_1_, bf16[512,768]{1,0:T(8,128)(2,1)} %collective-permute-done.2.refs_2_, ...), custom_call_target="tpu_custom_call" | custom-call | flops 3221225472 | bytes 9175040 | tf_op jit(solution)/shard_map/pallas_call | solution.py:56
  191.9 11.4 %all-to-all-start.2 = ((bf16[128,2,2048]{2,1,0:T(2,128)(2,1)}), bf16[128,2,2048]{2,1,0:T(2,128)(2,1)}, u32[]{:S(2)}, u32[]{:S(2)}) async-start(bf16[128,2,2048]{2,1,0:T(2,128)(2,1)} %reshape.45), calls=%async_computation.2 | async-start | bytes 2097152 | tf_op jit(solution)/shard_map/all_to_all | solution.py:228
  203.4 3.1 collective-permute-start.10
  206.5 3.4 collective-permute-start.9
  211.9 4.3 %collective-permute-start.7 = (bf16[256,512]{1,0:T(8,128)(2,1)S(1)}, bf16[256,512]{1,0:T(8,128)(2,1)S(1)}, u32[]{:S(2)}, u32[]{:S(2)}) collective-permute-start(bf16[256,512]{1,0:T(8,128)(2,1)S(1)} %get-tuple-element.18), channel_id=1, source_target_pairs={{0,256},{128,384},{256,0},{384,128},{1,257},{129,385},{257,1},{385... | collective-permute-start | bytes 786440 | tf_op jit(solution)/shard_map/ppermute | solution.py:13
  216.3 3.1 collective-permute-start.6
  219.3 5.4 %collective-permute-done.10 = bf16[256,1536]{1,0:T(8,128)(2,1)} collective-permute-done((bf16[256,1536]{1,0:T(8,128)(2,1)S(1)}, bf16[256,1536]{1,0:T(8,128)(2,1)}, u32[]{:S(2)}, u32[]{:S(2)}) %collective-permute-start.10) | collective-permute-done | bytes 786464 | tf_op jit(solution)/shard_map/ppermute | solution.py:13
  228.8 4.8 %collective-permute-start.12 = (bf16[128,1536]{1,0:T(8,128)(2,1)S(1)}, bf16[128,1536]{1,0:T(8,128)(2,1)S(1)}, u32[]{:S(2)}, u32[]{:S(2)}) collective-permute-start(bf16[128,1536]{1,0:T(8,128)(2,1)S(1)} %slice.39), channel_id=1, source_target_pairs={{0,384},{128,0},{256,128},{384,256},{1,385},{129,1},{257,129},{385... | collective-permute-start | bytes 1179656 | tf_op jit(solution)/shard_map/ppermute | solution.py:13
  234.7 10.0 %collective-permute-done.11 = bf16[128,1536]{1,0:T(8,128)(2,1)S(1)} collective-permute-done((bf16[128,1536]{1,0:T(8,128)(2,1)S(1)}, bf16[128,1536]{1,0:T(8,128)(2,1)S(1)}, u32[]{:S(2)}, u32[]{:S(2)}) %collective-permute-start.11) | collective-permute-done | bytes 393248 | tf_op jit(solution)/shard_map/ppermute | solution.py:13
  247.3 3.0 convolution_convert_fusion.1
  250.3 3.6 %reshape.47 = bf16[128,4,2,768]{3,2,1,0:T(2,128)(2,1)S(1)} reshape(bf16[512,1536]{1,0:T(8,128)(2,1)} %convolution_convert_fusion.1) | data formatting | bytes 3145728 | tf_op jit(solution)/shard_map/reshape | solution.py:248
  254.5 90.1 %shard_map.78 = bf16[128,2,4,768]{3,2,1,0:T(4,128)(2,1)S(1)} custom-call(bf16[128,2,4,768]{3,2,1,0:T(4,128)(2,1)S(1)} %bitcast.20), custom_call_target="tpu_custom_call" | custom-call | tf_op jit(solution)/shard_map/pallas_call | solution.py:163
  (63 shorter events, 33.1 us)
Async XLA Ops:
  5.4 20.7 %copy-start.8 = (s32[128,1]{0,1:T(1,128)S(1)}, s32[128,1]{0,1:T(1,128)}, u32[]{:S(2)}) copy-start(s32[128,1]{0,1:T(1,128)} %param.9) | copy-start | bytes 1540
  5.4 21.2 %copy-start.7 = (bf16[128,1,768]{2,0,1:T(8,128)(2,1)S(1)}, bf16[128,1,768]{2,0,1:T(8,128)(2,1)}, u32[]{:S(2)}) copy-start(bf16[128,1,768]{2,0,1:T(8,128)(2,1)} %param.7) | copy-start | bytes 589828
  5.4 21.2 %copy-start.10 = (f32[128,1]{0,1:T(1,128)S(1)}, f32[128,1]{0,1:T(1,128)}, u32[]{:S(2)}) copy-start(f32[128,1]{0,1:T(1,128)} %param.8) | copy-start | bytes 1540
  5.4 21.3 %copy-start.6 = (bf16[128,2048]{1,0:T(8,128)(2,1)S(1)}, bf16[128,2048]{1,0:T(8,128)(2,1)}, u32[]{:S(2)}) copy-start(bf16[128,2048]{1,0:T(8,128)(2,1)} %param.6) | copy-start | bytes 1572868
  5.4 93.7 %all-to-all-start = ((bf16[128,2,4,768]{3,2,1,0:T(4,128)(2,1)}), bf16[128,2,4,768]{3,2,1,0:T(4,128)(2,1)S(1)}, u32[]{:S(2)}, u32[]{:S(2)}) async-start(bf16[128,2,4,768]{3,2,1,0:T(4,128)(2,1)} %copy.20), calls=%async_computation | async-start | bytes 3145728 | tf_op jit(solution)/shard_map/all_to_all | solution.py:196
  99.1 79.7 %all-to-all-start.1 = ((bf16[128,2,2816]{2,1,0:T(2,128)(2,1)}), bf16[128,2,2816]{2,1,0:T(2,128)(2,1)}, u32[]{:S(2)}, u32[]{:S(2)}) async-start(bf16[128,2,2816]{2,1,0:T(2,128)(2,1)} %reshape.43), calls=%async_computation.1 | async-start | bytes 2883584 | tf_op jit(solution)/shard_map/all_to_all | solution.py:223
  112.8 4.8 %copy-start.5 = (bf16[128,1,4,768]{3,2,1,0:T(4,128)(2,1)S(1)}, bf16[128,1,4,768]{3,2,1,0:T(4,128)(2,1)}, u32[]{:S(2)}) copy-start(bf16[128,1,4,768]{3,2,1,0:T(4,128)(2,1)} %get-tuple-element.14) | copy-start | bytes 2359300
  114.4 67.8 %copy-start.3 = (bf16[512,768]{1,0:T(8,128)(2,1)}, bf16[512,768]{1,0:T(8,128)(2,1)S(1)}, u32[]{:S(2)}) copy-start(bf16[512,768]{1,0:T(8,128)(2,1)S(1)} %reshape_squeeze.6.refs_0_) | copy-start | bytes 2359300
  114.4 21.4 %collective-permute-start.1 = (bf16[512,768]{1,0:T(8,128)(2,1)S(1)}, bf16[512,768]{1,0:T(8,128)(2,1)}, u32[]{:S(2)}, u32[]{:S(2)}) collective-permute-start(bf16[512,768]{1,0:T(8,128)(2,1)S(1)} %reshape_squeeze.6.refs_0_), channel_id=1, source_target_pairs={{0,128},{128,256},{256,384},{384,0},{1,129},{129,257},{257,385},{3... | collective-permute-start | bytes 2359304 | tf_op jit(solution)/shard_map/ppermute | solution.py:13
  118.6 20.1 %collective-permute-start.3 = (bf16[512,768]{1,0:T(8,128)(2,1)}, bf16[512,768]{1,0:T(8,128)(2,1)}, u32[]{:S(2)}, u32[]{:S(2)}) collective-permute-start(bf16[512,768]{1,0:T(8,128)(2,1)} %reshape_squeeze.7.refs_4_), channel_id=1, source_target_pairs={{0,384},{128,0},{256,128},{384,256},{1,385},{129,1},{257,129},{385... | collective-permute-start | bytes 2359304 | tf_op jit(solution)/shard_map/ppermute | solution.py:13
  122.0 60.2 %collective-permute-start = (bf16[512,768]{1,0:T(8,128)(2,1)S(1)}, bf16[512,768]{1,0:T(8,128)(2,1)}, u32[]{:S(2)}, u32[]{:S(2)}) collective-permute-start(bf16[512,768]{1,0:T(8,128)(2,1)S(1)} %reshape_squeeze.6.refs_0_), channel_id=1, source_target_pairs={{0,384},{128,0},{256,128},{384,256},{1,385},{129,1},{257,129},{385... | collective-permute-start | bytes 2359304 | tf_op jit(solution)/shard_map/ppermute | solution.py:13
  125.2 57.1 %collective-permute-start.5 = (bf16[512,768]{1,0:T(8,128)(2,1)}, bf16[512,768]{1,0:T(8,128)(2,1)}, u32[]{:S(2)}, u32[]{:S(2)}) collective-permute-start(bf16[512,768]{1,0:T(8,128)(2,1)} %reshape_squeeze.7.refs_4_), channel_id=1, source_target_pairs={{0,128},{128,256},{256,384},{384,0},{1,129},{129,257},{257,385},{3... | collective-permute-start | bytes 2359304 | tf_op jit(solution)/shard_map/ppermute | solution.py:13
  135.8 46.5 %collective-permute-start.2 = (bf16[512,768]{1,0:T(8,128)(2,1)}, bf16[512,768]{1,0:T(8,128)(2,1)}, u32[]{:S(2)}, u32[]{:S(2)}) collective-permute-start(bf16[512,768]{1,0:T(8,128)(2,1)} %collective-permute-done.1.refs_3_), channel_id=1, source_target_pairs={{0,128},{128,256},{256,384},{384,0},{1,129},{129,257},{257,385},{3... | collective-permute-start | bytes 2359304 | tf_op jit(solution)/shard_map/ppermute | solution.py:13
  138.7 43.6 %collective-permute-start.4 = (bf16[512,768]{1,0:T(8,128)(2,1)}, bf16[512,768]{1,0:T(8,128)(2,1)}, u32[]{:S(2)}, u32[]{:S(2)}) collective-permute-start(bf16[512,768]{1,0:T(8,128)(2,1)} %collective-permute-done.3.refs_5_), channel_id=1, source_target_pairs={{0,384},{128,0},{256,128},{384,256},{1,385},{129,1},{257,129},{385... | collective-permute-start | bytes 2359304 | tf_op jit(solution)/shard_map/ppermute | solution.py:13
  191.9 11.4 %copy-start.2 = (bf16[256,1536]{1,0:T(8,128)(2,1)S(1)}, bf16[256,1536]{1,0:T(8,128)(2,1)}, u32[]{:S(2)}) copy-start(bf16[256,1536]{1,0:T(8,128)(2,1)} %copy-done.1) | copy-start | bytes 2359300
  191.9 154.8 %all-to-all-start.2 = ((bf16[128,2,2048]{2,1,0:T(2,128)(2,1)}), bf16[128,2,2048]{2,1,0:T(2,128)(2,1)}, u32[]{:S(2)}, u32[]{:S(2)}) async-start(bf16[128,2,2048]{2,1,0:T(2,128)(2,1)} %reshape.45), calls=%async_computation.2 | async-start | bytes 2097152 | tf_op jit(solution)/shard_map/all_to_all | solution.py:228
  203.4 21.3 %collective-permute-start.10 = (bf16[256,1536]{1,0:T(8,128)(2,1)S(1)}, bf16[256,1536]{1,0:T(8,128)(2,1)}, u32[]{:S(2)}, u32[]{:S(2)}) collective-permute-start(bf16[256,1536]{1,0:T(8,128)(2,1)S(1)} %copy-done.2), channel_id=1, source_target_pairs={{0,128},{128,256},{256,384},{384,0},{1,129},{129,257},{257,385},{3... | collective-permute-start | bytes 2359304 | tf_op jit(solution)/shard_map/ppermute | solution.py:13
  206.5 21.2 %collective-permute-start.9 = (bf16[256,1536]{1,0:T(8,128)(2,1)S(1)}, bf16[256,1536]{1,0:T(8,128)(2,1)}, u32[]{:S(2)}, u32[]{:S(2)}) collective-permute-start(bf16[256,1536]{1,0:T(8,128)(2,1)S(1)} %copy-done.2), channel_id=1, source_target_pairs={{0,384},{128,0},{256,128},{384,256},{1,385},{129,1},{257,129},{385... | collective-permute-start | bytes 2359304 | tf_op jit(solution)/shard_map/ppermute | solution.py:13
  210.0 37.3 %collective-permute-start.8 = (bf16[256,512]{1,0:T(8,128)(2,1)S(1)}, bf16[256,512]{1,0:T(8,128)(2,1)S(1)}, u32[]{:S(2)}, u32[]{:S(2)}) collective-permute-start(bf16[256,512]{1,0:T(8,128)(2,1)S(1)} %get-tuple-element.17), channel_id=1, source_target_pairs={{0,128},{128,256},{256,384},{384,0},{1,129},{129,257},{257,385},{3... | collective-permute-start | bytes 786440 | tf_op jit(solution)/shard_map/ppermute | solution.py:13
  211.9 35.4 %collective-permute-start.7 = (bf16[256,512]{1,0:T(8,128)(2,1)S(1)}, bf16[256,512]{1,0:T(8,128)(2,1)S(1)}, u32[]{:S(2)}, u32[]{:S(2)}) collective-permute-start(bf16[256,512]{1,0:T(8,128)(2,1)S(1)} %get-tuple-element.18), channel_id=1, source_target_pairs={{0,256},{128,384},{256,0},{384,128},{1,257},{129,385},{257,1},{385... | collective-permute-start | bytes 786440 | tf_op jit(solution)/shard_map/ppermute | solution.py:13
  216.3 31.0 %collective-permute-start.6 = (bf16[256,512]{1,0:T(8,128)(2,1)S(1)}, bf16[256,512]{1,0:T(8,128)(2,1)S(1)}, u32[]{:S(2)}, u32[]{:S(2)}) collective-permute-start(bf16[256,512]{1,0:T(8,128)(2,1)S(1)} %get-tuple-element.19), channel_id=1, source_target_pairs={{0,384},{128,0},{256,128},{384,256},{1,385},{129,1},{257,129},{385... | collective-permute-start | bytes 786440 | tf_op jit(solution)/shard_map/ppermute | solution.py:13
  225.7 19.0 %collective-permute-start.11 = (bf16[128,1536]{1,0:T(8,128)(2,1)S(1)}, bf16[128,1536]{1,0:T(8,128)(2,1)S(1)}, u32[]{:S(2)}, u32[]{:S(2)}) collective-permute-start(bf16[128,1536]{1,0:T(8,128)(2,1)S(1)} %slice.38), channel_id=1, source_target_pairs={{0,128},{128,256},{256,384},{384,0},{1,129},{129,257},{257,385},{3... | collective-permute-start | bytes 1179656 | tf_op jit(solution)/shard_map/ppermute | solution.py:13
  228.8 17.3 %collective-permute-start.12 = (bf16[128,1536]{1,0:T(8,128)(2,1)S(1)}, bf16[128,1536]{1,0:T(8,128)(2,1)S(1)}, u32[]{:S(2)}, u32[]{:S(2)}) collective-permute-start(bf16[128,1536]{1,0:T(8,128)(2,1)S(1)} %slice.39), channel_id=1, source_target_pairs={{0,384},{128,0},{256,128},{384,256},{1,385},{129,1},{257,129},{385... | collective-permute-start | bytes 1179656 | tf_op jit(solution)/shard_map/ppermute | solution.py:13
  254.5 90.1 %copy-start.9 = (s32[128]{0:T(128)S(1)}, s32[128]{0:T(128)}, u32[]{:S(2)}) copy-start(s32[128]{0:T(128)} %param.10) | copy-start | bytes 1540
  (3 other events, 3.2 us)

commit v4 on v3

--- a/solution.py
+++ b/solution.py
@@ -239,12 +239,20 @@
     grads_right = shift(grads, -1)
     middle = depth_rows // 2
     grads_far = [shift(grads_left[:middle], 1), shift(grads_right[middle:], -1)]
-    all_columns = jnp.concatenate(columns, axis=0)
-    all_grads = jnp.concatenate([grads, grads_right, *grads_far, grads_left], axis=0)
     contract_rows = (((0,), (0,)), ((), ()))
-    summed = lax.dot_general(
-        all_columns, all_grads, contract_rows, preferred_element_type=jnp.float32
-    ).astype(jnp.bfloat16)
+    own_columns, right_columns, far_columns, left_columns = columns
+    summed = jnp.float32(0.0)
+    for column, grad in (
+        (own_columns, grads),
+        (left_columns, grads_left),
+        (right_columns, grads_right),
+        (far_columns[:middle], grads_far[0]),
+        (far_columns[middle:], grads_far[1]),
+    ):
+        summed = lax.optimization_barrier(summed) + lax.dot_general(
+            column, grad, contract_rows, preferred_element_type=jnp.float32
+        )
+    summed = summed.astype(jnp.bfloat16)
     pieces = summed.reshape(expert_count, shard_rows, 2, hidden_width).transpose(0, 2, 1, 3)
     gathered = exchange(pieces)
     membership = one_hot(

time: 351 us -> 349 us (level)
  waiting for transfers between devices: 128 us -> 124 us
    ppermute x13, waiting for transfers between devices: 26.1 us -> 21.9 us  [shift(): lax.ppermute(values, 'dp', [(i, (i + distance) % size) for i in range(siz...]
  transfers between devices with their start and end apart: 16 -> 16, of which waited for: 7 -> 7; matrix products, arithmetic and copies ran while one was open for 8% -> 9% of each run, Pallas kernels for 26% -> 26%
where the time goes in v4:
time: 349 us; the launch traced here: 348 us
  waiting for transfers between devices  124 us (36%)
  Pallas kernels  95.9 us (27%)
  starting transfers between devices  84.5 us (24%)
  local copies, waits for them, and re-layouts  28.3 us (8%)
  matrix products  8.99 us (3%)
  other arithmetic  5.19 us (1%)
    pallas_call x1, Pallas kernels, exchange(): pl.pallas_call(functools.partial(exchange_kernel, total), out_shape=jax.S...  89.8 us
    all_to_all x1, waiting for transfers between devices, per_device(): lax.all_to_all(send_weights, 'expert', split_axis=0, concat_axis=0, tiled...  66.2 us
    ppermute x13, starting transfers between devices, shift(): lax.ppermute(values, 'dp', [(i, (i + distance) % size) for i in range(siz...  40.4 us
    all_to_all x1, waiting for transfers between devices, per_device(): lax.all_to_all(send_rows, 'expert', split_axis=0, concat_axis=0, tiled=True)  35.4 us
    ppermute x13, waiting for transfers between devices, shift(): lax.ppermute(values, 'dp', [(i, (i + distance) % size) for i in range(siz...  21.9 us
    all_to_all x1, starting transfers between devices, per_device(): lax.all_to_all(send_weights, 'expert', split_axis=0, concat_axis=0, tiled...  20.7 us
    all_to_all x1, starting transfers between devices, per_device(): lax.all_to_all(send_rows, 'expert', split_axis=0, concat_axis=0, tiled=True)  12 us
    all_to_all x1, starting transfers between devices, per_device(): lax.all_to_all(row_terms.reshape(expert_count, capacity, model_width), 'e...  11.4 us
  transfers between devices with their start and end apart: 16, of which 7 were waited for; matrix products, arithmetic and copies ran while one was open for 9% of the time, Pallas kernels for 26%

profile of v4, /device:TPU:1, one launch (start us, length us, event | category | flops | bytes accessed | tf_op | source)
XLA Modules:
  0.0 347.5 jit_solution(12107906646994970718)
XLA Ops:
  3.0 2.3 copy.20
  5.4 20.7 %all-to-all-start = ((bf16[128,2,4,768]{3,2,1,0:T(4,128)(2,1)}), bf16[128,2,4,768]{3,2,1,0:T(4,128)(2,1)S(1)}, u32[]{:S(2)}, u32[]{:S(2)}) async-start(bf16[128,2,4,768]{3,2,1,0:T(4,128)(2,1)} %copy.20), calls=%async_computation | async-start | bytes 3145728 | tf_op jit(solution)/shard_map/all_to_all | solution.py:196
  28.6 4.2 %reshape.43 = bf16[128,2,2816]{2,1,0:T(2,128)(2,1)} reshape(bf16[256,2816]{1,0:T(8,128)(2,1)} %convolution_convert_fusion) | data formatting | bytes 2883584 | tf_op jit(solution)/shard_map/reshape | solution.py:221
  32.8 66.2 %all-to-all-done = bf16[128,2,4,768]{3,2,1,0:T(4,128)(2,1)S(1)} async-done(((bf16[128,2,4,768]{3,2,1,0:T(4,128)(2,1)}), bf16[128,2,4,768]{3,2,1,0:T(4,128)(2,1)S(1)}, u32[]{:S(2)}, u32[]{:S(2)}) %all-to-all-start) | async-done | bytes 1572896 | tf_op jit(solution)/shard_map/all_to_all | solution.py:196
  99.1 12.0 %all-to-all-start.1 = ((bf16[128,2,2816]{2,1,0:T(2,128)(2,1)}), bf16[128,2,2816]{2,1,0:T(2,128)(2,1)}, u32[]{:S(2)}, u32[]{:S(2)}) async-start(bf16[128,2,2816]{2,1,0:T(2,128)(2,1)} %reshape.43), calls=%async_computation.1 | async-start | bytes 2883584 | tf_op jit(solution)/shard_map/all_to_all | solution.py:223
  114.4 3.1 collective-permute-start.1
  118.6 3.4 collective-permute-start.3
  122.0 3.2 collective-permute-start
  125.2 2.1 collective-permute-start.5
  127.3 8.5 %collective-permute-done.1.refs_3_ = bf16[512,768]{1,0:T(8,128)(2,1)} collective-permute-done((bf16[512,768]{1,0:T(8,128)(2,1)S(1)}, bf16[512,768]{1,0:T(8,128)(2,1)}, u32[]{:S(2)}, u32[]{:S(2)}) %collective-permute-start.1) | collective-permute-done | bytes 786464 | tf_op jit(solution)/shard_map/ppermute | solution.py:13
  138.7 4.8 %collective-permute-start.4 = (bf16[512,768]{1,0:T(8,128)(2,1)}, bf16[512,768]{1,0:T(8,128)(2,1)}, u32[]{:S(2)}, u32[]{:S(2)}) collective-permute-start(bf16[512,768]{1,0:T(8,128)(2,1)} %collective-permute-done.3.refs_5_), channel_id=1, source_target_pairs={{0,384},{128,0},{256,128},{384,256},{1,385},{129,1},{257,129},{385... | collective-permute-start | bytes 2359304 | tf_op jit(solution)/shard_map/ppermute | solution.py:13
  143.5 35.4 %all-to-all-done.1 = bf16[128,2,2816]{2,1,0:T(2,128)(2,1)} async-done(((bf16[128,2,2816]{2,1,0:T(2,128)(2,1)}), bf16[128,2,2816]{2,1,0:T(2,128)(2,1)}, u32[]{:S(2)}, u32[]{:S(2)}) %all-to-all-start.1) | async-done | bytes 1441824 | tf_op jit(solution)/shard_map/all_to_all | solution.py:223
  178.8 3.4 reshape.44.rows_ref
  183.4 6.1 %shard_map.77 = (bf16[256,1536]{1,0:T(8,128)(2,1)S(1)}, bf16[256,2048]{1,0:T(8,128)(2,1)S(1)}) custom-call(bf16[256,2816]{1,0:T(8,128)(2,1)S(1)} %reshape.44.rows_ref, bf16[512,768]{1,0:T(8,128)(2,1)S(1)} %copy-done.4, bf16[512,768]{1,0:T(8,128)(2,1)} %collective-permute-done.refs_1_, bf16[512,768]{1,0:T(8,128)(2,1)} %collective-permute-done.2.refs_2_, ...), custom_call_target="tpu_custom_call" | custom-call | flops 3221225472 | bytes 9175040 | tf_op jit(solution)/shard_map/pallas_call | solution.py:56
  191.9 11.4 %all-to-all-start.2 = ((bf16[128,2,2048]{2,1,0:T(2,128)(2,1)}), bf16[128,2,2048]{2,1,0:T(2,128)(2,1)}, u32[]{:S(2)}, u32[]{:S(2)}) async-start(bf16[128,2,2048]{2,1,0:T(2,128)(2,1)} %reshape.45), calls=%async_computation.2 | async-start | bytes 2097152 | tf_op jit(solution)/shard_map/all_to_all | solution.py:228
  203.4 3.1 collective-permute-start.7
  206.5 3.4 collective-permute-start.9
  212.5 4.6 %collective-permute-start.8 = (bf16[256,512]{1,0:T(8,128)(2,1)S(1)}, bf16[256,512]{1,0:T(8,128)(2,1)S(1)}, u32[]{:S(2)}, u32[]{:S(2)}) collective-permute-start(bf16[256,512]{1,0:T(8,128)(2,1)S(1)} %get-tuple-element.17), channel_id=1, source_target_pairs={{0,384},{128,0},{256,128},{384,256},{1,385},{129,1},{257,129},{385... | collective-permute-start | bytes 786440 | tf_op jit(solution)/shard_map/ppermute | solution.py:13
  217.1 2.2 collective-permute-start.10
  219.3 5.4 %collective-permute-done.7 = bf16[256,1536]{1,0:T(8,128)(2,1)} collective-permute-done((bf16[256,1536]{1,0:T(8,128)(2,1)S(1)}, bf16[256,1536]{1,0:T(8,128)(2,1)}, u32[]{:S(2)}, u32[]{:S(2)}) %collective-permute-start.7) | collective-permute-done | bytes 786464 | tf_op jit(solution)/shard_map/ppermute | solution.py:13
  228.7 4.8 %collective-permute-start.12 = (bf16[128,1536]{1,0:T(8,128)(2,1)S(1)}, bf16[128,1536]{1,0:T(8,128)(2,1)S(1)}, u32[]{:S(2)}, u32[]{:S(2)}) collective-permute-start(bf16[128,1536]{1,0:T(8,128)(2,1)S(1)} %slice.49), channel_id=1, source_target_pairs={{0,384},{128,0},{256,128},{384,256},{1,385},{129,1},{257,129},{385... | collective-permute-start | bytes 1179656 | tf_op jit(solution)/shard_map/ppermute | solution.py:13
  238.1 6.6 %collective-permute-done.11 = bf16[128,1536]{1,0:T(8,128)(2,1)S(1)} collective-permute-done((bf16[128,1536]{1,0:T(8,128)(2,1)S(1)}, bf16[128,1536]{1,0:T(8,128)(2,1)S(1)}, u32[]{:S(2)}, u32[]{:S(2)}) %collective-permute-start.11) | collective-permute-done | bytes 393248 | tf_op jit(solution)/shard_map/ppermute | solution.py:13
  248.5 3.6 %reshape.47 = bf16[128,4,2,768]{3,2,1,0:T(2,128)(2,1)S(1)} reshape(bf16[512,1536]{1,0:T(8,128)(2,1)} %add_convert_fusion) | data formatting | bytes 3145728 | tf_op jit(solution)/shard_map/reshape | solution.py:256
  252.8 89.8 %shard_map.78 = bf16[128,2,4,768]{3,2,1,0:T(4,128)(2,1)S(1)} custom-call(bf16[128,2,4,768]{3,2,1,0:T(4,128)(2,1)S(1)} %bitcast.26), custom_call_target="tpu_custom_call" | custom-call | tf_op jit(solution)/shard_map/pallas_call | solution.py:163
  (66 shorter events, 36.1 us)
Async XLA Ops:
  5.4 20.7 %copy-start.8 = (s32[128,1]{0,1:T(1,128)S(1)}, s32[128,1]{0,1:T(1,128)}, u32[]{:S(2)}) copy-start(s32[128,1]{0,1:T(1,128)} %param.9) | copy-start | bytes 1540
  5.4 21.2 %copy-start.7 = (bf16[128,1,768]{2,0,1:T(8,128)(2,1)S(1)}, bf16[128,1,768]{2,0,1:T(8,128)(2,1)}, u32[]{:S(2)}) copy-start(bf16[128,1,768]{2,0,1:T(8,128)(2,1)} %param.7) | copy-start | bytes 589828
  5.4 21.2 %copy-start.10 = (f32[128,1]{0,1:T(1,128)S(1)}, f32[128,1]{0,1:T(1,128)}, u32[]{:S(2)}) copy-start(f32[128,1]{0,1:T(1,128)} %param.8) | copy-start | bytes 1540
  5.4 21.3 %copy-start.6 = (bf16[128,2048]{1,0:T(8,128)(2,1)S(1)}, bf16[128,2048]{1,0:T(8,128)(2,1)}, u32[]{:S(2)}) copy-start(bf16[128,2048]{1,0:T(8,128)(2,1)} %param.6) | copy-start | bytes 1572868
  5.4 93.7 %all-to-all-start = ((bf16[128,2,4,768]{3,2,1,0:T(4,128)(2,1)}), bf16[128,2,4,768]{3,2,1,0:T(4,128)(2,1)S(1)}, u32[]{:S(2)}, u32[]{:S(2)}) async-start(bf16[128,2,4,768]{3,2,1,0:T(4,128)(2,1)} %copy.20), calls=%async_computation | async-start | bytes 3145728 | tf_op jit(solution)/shard_map/all_to_all | solution.py:196
  99.1 79.7 %all-to-all-start.1 = ((bf16[128,2,2816]{2,1,0:T(2,128)(2,1)}), bf16[128,2,2816]{2,1,0:T(2,128)(2,1)}, u32[]{:S(2)}, u32[]{:S(2)}) async-start(bf16[128,2,2816]{2,1,0:T(2,128)(2,1)} %reshape.43), calls=%async_computation.1 | async-start | bytes 2883584 | tf_op jit(solution)/shard_map/all_to_all | solution.py:223
  112.8 4.8 %copy-start.5 = (bf16[128,1,4,768]{3,2,1,0:T(4,128)(2,1)S(1)}, bf16[128,1,4,768]{3,2,1,0:T(4,128)(2,1)}, u32[]{:S(2)}) copy-start(bf16[128,1,4,768]{3,2,1,0:T(4,128)(2,1)} %get-tuple-element.14) | copy-start | bytes 2359300
  114.4 67.8 %copy-start.3 = (bf16[512,768]{1,0:T(8,128)(2,1)}, bf16[512,768]{1,0:T(8,128)(2,1)S(1)}, u32[]{:S(2)}) copy-start(bf16[512,768]{1,0:T(8,128)(2,1)S(1)} %reshape_squeeze.6.refs_0_) | copy-start | bytes 2359300
  114.4 21.4 %collective-permute-start.1 = (bf16[512,768]{1,0:T(8,128)(2,1)S(1)}, bf16[512,768]{1,0:T(8,128)(2,1)}, u32[]{:S(2)}, u32[]{:S(2)}) collective-permute-start(bf16[512,768]{1,0:T(8,128)(2,1)S(1)} %reshape_squeeze.6.refs_0_), channel_id=1, source_target_pairs={{0,128},{128,256},{256,384},{384,0},{1,129},{129,257},{257,385},{3... | collective-permute-start | bytes 2359304 | tf_op jit(solution)/shard_map/ppermute | solution.py:13
  118.6 20.1 %collective-permute-start.3 = (bf16[512,768]{1,0:T(8,128)(2,1)}, bf16[512,768]{1,0:T(8,128)(2,1)}, u32[]{:S(2)}, u32[]{:S(2)}) collective-permute-start(bf16[512,768]{1,0:T(8,128)(2,1)} %reshape_squeeze.7.refs_4_), channel_id=1, source_target_pairs={{0,384},{128,0},{256,128},{384,256},{1,385},{129,1},{257,129},{385... | collective-permute-start | bytes 2359304 | tf_op jit(solution)/shard_map/ppermute | solution.py:13
  122.0 60.2 %collective-permute-start = (bf16[512,768]{1,0:T(8,128)(2,1)S(1)}, bf16[512,768]{1,0:T(8,128)(2,1)}, u32[]{:S(2)}, u32[]{:S(2)}) collective-permute-start(bf16[512,768]{1,0:T(8,128)(2,1)S(1)} %reshape_squeeze.6.refs_0_), channel_id=1, source_target_pairs={{0,384},{128,0},{256,128},{384,256},{1,385},{129,1},{257,129},{385... | collective-permute-start | bytes 2359304 | tf_op jit(solution)/shard_map/ppermute | solution.py:13
  125.2 57.1 %collective-permute-start.5 = (bf16[512,768]{1,0:T(8,128)(2,1)}, bf16[512,768]{1,0:T(8,128)(2,1)}, u32[]{:S(2)}, u32[]{:S(2)}) collective-permute-start(bf16[512,768]{1,0:T(8,128)(2,1)} %reshape_squeeze.7.refs_4_), channel_id=1, source_target_pairs={{0,128},{128,256},{256,384},{384,0},{1,129},{129,257},{257,385},{3... | collective-permute-start | bytes 2359304 | tf_op jit(solution)/shard_map/ppermute | solution.py:13
  135.8 46.5 %collective-permute-start.2 = (bf16[512,768]{1,0:T(8,128)(2,1)}, bf16[512,768]{1,0:T(8,128)(2,1)}, u32[]{:S(2)}, u32[]{:S(2)}) collective-permute-start(bf16[512,768]{1,0:T(8,128)(2,1)} %collective-permute-done.1.refs_3_), channel_id=1, source_target_pairs={{0,128},{128,256},{256,384},{384,0},{1,129},{129,257},{257,385},{3... | collective-permute-start | bytes 2359304 | tf_op jit(solution)/shard_map/ppermute | solution.py:13
  138.7 43.6 %collective-permute-start.4 = (bf16[512,768]{1,0:T(8,128)(2,1)}, bf16[512,768]{1,0:T(8,128)(2,1)}, u32[]{:S(2)}, u32[]{:S(2)}) collective-permute-start(bf16[512,768]{1,0:T(8,128)(2,1)} %collective-permute-done.3.refs_5_), channel_id=1, source_target_pairs={{0,384},{128,0},{256,128},{384,256},{1,385},{129,1},{257,129},{385... | collective-permute-start | bytes 2359304 | tf_op jit(solution)/shard_map/ppermute | solution.py:13
  191.9 11.4 %copy-start.2 = (bf16[256,1536]{1,0:T(8,128)(2,1)S(1)}, bf16[256,1536]{1,0:T(8,128)(2,1)}, u32[]{:S(2)}) copy-start(bf16[256,1536]{1,0:T(8,128)(2,1)} %copy-done.1) | copy-start | bytes 2359300
  191.9 152.7 %all-to-all-start.2 = ((bf16[128,2,2048]{2,1,0:T(2,128)(2,1)}), bf16[128,2,2048]{2,1,0:T(2,128)(2,1)}, u32[]{:S(2)}, u32[]{:S(2)}) async-start(bf16[128,2,2048]{2,1,0:T(2,128)(2,1)} %reshape.45), calls=%async_computation.2 | async-start | bytes 2097152 | tf_op jit(solution)/shard_map/all_to_all | solution.py:228
  203.4 21.3 %collective-permute-start.7 = (bf16[256,1536]{1,0:T(8,128)(2,1)S(1)}, bf16[256,1536]{1,0:T(8,128)(2,1)}, u32[]{:S(2)}, u32[]{:S(2)}) collective-permute-start(bf16[256,1536]{1,0:T(8,128)(2,1)S(1)} %copy-done.2), channel_id=1, source_target_pairs={{0,128},{128,256},{256,384},{384,0},{1,129},{129,257},{257,385},{3... | collective-permute-start | bytes 2359304 | tf_op jit(solution)/shard_map/ppermute | solution.py:13
  206.5 21.2 %collective-permute-start.9 = (bf16[256,1536]{1,0:T(8,128)(2,1)S(1)}, bf16[256,1536]{1,0:T(8,128)(2,1)}, u32[]{:S(2)}, u32[]{:S(2)}) collective-permute-start(bf16[256,1536]{1,0:T(8,128)(2,1)S(1)} %copy-done.2), channel_id=1, source_target_pairs={{0,384},{128,0},{256,128},{384,256},{1,385},{129,1},{257,129},{385... | collective-permute-start | bytes 2359304 | tf_op jit(solution)/shard_map/ppermute | solution.py:13
  210.0 23.5 %collective-permute-start.6 = (bf16[256,512]{1,0:T(8,128)(2,1)S(1)}, bf16[256,512]{1,0:T(8,128)(2,1)S(1)}, u32[]{:S(2)}, u32[]{:S(2)}) collective-permute-start(bf16[256,512]{1,0:T(8,128)(2,1)S(1)} %get-tuple-element.18), channel_id=1, source_target_pairs={{0,128},{128,256},{256,384},{384,0},{1,129},{129,257},{257,385},{3... | collective-permute-start | bytes 786440 | tf_op jit(solution)/shard_map/ppermute | solution.py:13
  212.5 22.7 %collective-permute-start.8 = (bf16[256,512]{1,0:T(8,128)(2,1)S(1)}, bf16[256,512]{1,0:T(8,128)(2,1)S(1)}, u32[]{:S(2)}, u32[]{:S(2)}) collective-permute-start(bf16[256,512]{1,0:T(8,128)(2,1)S(1)} %get-tuple-element.17), channel_id=1, source_target_pairs={{0,384},{128,0},{256,128},{384,256},{1,385},{129,1},{257,129},{385... | collective-permute-start | bytes 786440 | tf_op jit(solution)/shard_map/ppermute | solution.py:13
  217.1 21.1 %collective-permute-start.10 = (bf16[256,512]{1,0:T(8,128)(2,1)S(1)}, bf16[256,512]{1,0:T(8,128)(2,1)S(1)}, u32[]{:S(2)}, u32[]{:S(2)}) collective-permute-start(bf16[256,512]{1,0:T(8,128)(2,1)S(1)} %get-tuple-element.16), channel_id=1, source_target_pairs={{0,256},{128,384},{256,0},{384,128},{1,257},{129,385},{257,1},{385... | collective-permute-start | bytes 786440 | tf_op jit(solution)/shard_map/ppermute | solution.py:13
  225.7 19.0 %collective-permute-start.11 = (bf16[128,1536]{1,0:T(8,128)(2,1)S(1)}, bf16[128,1536]{1,0:T(8,128)(2,1)S(1)}, u32[]{:S(2)}, u32[]{:S(2)}) collective-permute-start(bf16[128,1536]{1,0:T(8,128)(2,1)S(1)} %slice.47), channel_id=1, source_target_pairs={{0,128},{128,256},{256,384},{384,0},{1,129},{129,257},{257,385},{3... | collective-permute-start | bytes 1179656 | tf_op jit(solution)/shard_map/ppermute | solution.py:13
  228.7 17.6 %collective-permute-start.12 = (bf16[128,1536]{1,0:T(8,128)(2,1)S(1)}, bf16[128,1536]{1,0:T(8,128)(2,1)S(1)}, u32[]{:S(2)}, u32[]{:S(2)}) collective-permute-start(bf16[128,1536]{1,0:T(8,128)(2,1)S(1)} %slice.49), channel_id=1, source_target_pairs={{0,384},{128,0},{256,128},{384,256},{1,385},{129,1},{257,129},{385... | collective-permute-start | bytes 1179656 | tf_op jit(solution)/shard_map/ppermute | solution.py:13
  252.8 89.8 %copy-start.9 = (s32[128]{0:T(128)S(1)}, s32[128]{0:T(128)}, u32[]{:S(2)}) copy-start(s32[128]{0:T(128)} %param.10) | copy-start | bytes 1540
  (3 other events, 3.2 us)

commit v5 on v4

--- a/solution.py
+++ b/solution.py
@@ -133,7 +133,7 @@
         return carry
 
     pairs = (planes // 2 - 1) * PLANE
-    lax.fori_loop(0, pairs // 2, both_ways, 0)
+    lax.fori_loop(0, pairs // 4, both_ways, 0)
     relay.wait_recv()
     source = device(planes // 4, seat)
     for place in range(half):
@@ -145,7 +145,7 @@
             device_id={"expert": device(-(planes // 4), half + place)},
             device_id_type=pl.DeviceIdType.MESH,
         ).start()
-    lax.fori_loop(pairs // 2, pairs, both_ways, 0)
+    lax.fori_loop(pairs // 4, pairs, both_ways, 0)
     lax.fori_loop(1, PLANE, same_plane, 0)
 
     own.wait()

time: 349 us -> 349 us (level)
  no operation moved by 1% of the time
where the time goes in v5:
time: 349 us; the launch traced here: 348 us
  waiting for transfers between devices  124 us (36%)
  Pallas kernels  95.9 us (27%)
  starting transfers between devices  84.5 us (24%)
  local copies, waits for them, and re-layouts  28.3 us (8%)
  matrix products  8.99 us (3%)
  other arithmetic  5.19 us (1%)
    pallas_call x1, Pallas kernels, exchange(): pl.pallas_call(functools.partial(exchange_kernel, total), out_shape=jax.S...  89.8 us
    all_to_all x1, waiting for transfers between devices, per_device(): lax.all_to_all(send_weights, 'expert', split_axis=0, concat_axis=0, tiled...  66.2 us
    ppermute x13, starting transfers between devices, shift(): lax.ppermute(values, 'dp', [(i, (i + distance) % size) for i in range(siz...  40.4 us
    all_to_all x1, waiting for transfers between devices, per_device(): lax.all_to_all(send_rows, 'expert', split_axis=0, concat_axis=0, tiled=True)  35.4 us
    ppermute x13, waiting for transfers between devices, shift(): lax.ppermute(values, 'dp', [(i, (i + distance) % size) for i in range(siz...  21.9 us
    all_to_all x1, starting transfers between devices, per_device(): lax.all_to_all(send_weights, 'expert', split_axis=0, concat_axis=0, tiled...  20.7 us
    all_to_all x1, starting transfers between devices, per_device(): lax.all_to_all(send_rows, 'expert', split_axis=0, concat_axis=0, tiled=True)  12 us
    all_to_all x1, starting transfers between devices, per_device(): lax.all_to_all(row_terms.reshape(expert_count, capacity, model_width), 'e...  11.4 us
  transfers between devices with their start and end apart: 16, of which 7 were waited for; matrix products, arithmetic and copies ran while one was open for 9% of the time, Pallas kernels for 26%

profile of v5, /device:TPU:1, one launch (start us, length us, event | category | flops | bytes accessed | tf_op | source)
XLA Modules:
  0.0 347.5 jit_solution(11424315277322060477)
XLA Ops:
  3.0 2.3 copy.20
  5.4 20.7 %all-to-all-start = ((bf16[128,2,4,768]{3,2,1,0:T(4,128)(2,1)}), bf16[128,2,4,768]{3,2,1,0:T(4,128)(2,1)S(1)}, u32[]{:S(2)}, u32[]{:S(2)}) async-start(bf16[128,2,4,768]{3,2,1,0:T(4,128)(2,1)} %copy.20), calls=%async_computation | async-start | bytes 3145728 | tf_op jit(solution)/shard_map/all_to_all | solution.py:196
  28.6 4.2 %reshape.43 = bf16[128,2,2816]{2,1,0:T(2,128)(2,1)} reshape(bf16[256,2816]{1,0:T(8,128)(2,1)} %convolution_convert_fusion) | data formatting | bytes 2883584 | tf_op jit(solution)/shard_map/reshape | solution.py:221
  32.8 66.2 %all-to-all-done = bf16[128,2,4,768]{3,2,1,0:T(4,128)(2,1)S(1)} async-done(((bf16[128,2,4,768]{3,2,1,0:T(4,128)(2,1)}), bf16[128,2,4,768]{3,2,1,0:T(4,128)(2,1)S(1)}, u32[]{:S(2)}, u32[]{:S(2)}) %all-to-all-start) | async-done | bytes 1572896 | tf_op jit(solution)/shard_map/all_to_all | solution.py:196
  99.1 12.0 %all-to-all-start.1 = ((bf16[128,2,2816]{2,1,0:T(2,128)(2,1)}), bf16[128,2,2816]{2,1,0:T(2,128)(2,1)}, u32[]{:S(2)}, u32[]{:S(2)}) async-start(bf16[128,2,2816]{2,1,0:T(2,128)(2,1)} %reshape.43), calls=%async_computation.1 | async-start | bytes 2883584 | tf_op jit(solution)/shard_map/all_to_all | solution.py:223
  114.4 3.1 collective-permute-start.1
  118.6 3.4 collective-permute-start.3
  122.0 3.2 collective-permute-start
  125.2 2.1 collective-permute-start.5
  127.3 8.5 %collective-permute-done.1.refs_3_ = bf16[512,768]{1,0:T(8,128)(2,1)} collective-permute-done((bf16[512,768]{1,0:T(8,128)(2,1)S(1)}, bf16[512,768]{1,0:T(8,128)(2,1)}, u32[]{:S(2)}, u32[]{:S(2)}) %collective-permute-start.1) | collective-permute-done | bytes 786464 | tf_op jit(solution)/shard_map/ppermute | solution.py:13
  138.7 4.8 %collective-permute-start.4 = (bf16[512,768]{1,0:T(8,128)(2,1)}, bf16[512,768]{1,0:T(8,128)(2,1)}, u32[]{:S(2)}, u32[]{:S(2)}) collective-permute-start(bf16[512,768]{1,0:T(8,128)(2,1)} %collective-permute-done.3.refs_5_), channel_id=1, source_target_pairs={{0,384},{128,0},{256,128},{384,256},{1,385},{129,1},{257,129},{385... | collective-permute-start | bytes 2359304 | tf_op jit(solution)/shard_map/ppermute | solution.py:13
  143.5 35.4 %all-to-all-done.1 = bf16[128,2,2816]{2,1,0:T(2,128)(2,1)} async-done(((bf16[128,2,2816]{2,1,0:T(2,128)(2,1)}), bf16[128,2,2816]{2,1,0:T(2,128)(2,1)}, u32[]{:S(2)}, u32[]{:S(2)}) %all-to-all-start.1) | async-done | bytes 1441824 | tf_op jit(solution)/shard_map/all_to_all | solution.py:223
  178.8 3.4 reshape.44.rows_ref
  183.4 6.1 %shard_map.77 = (bf16[256,1536]{1,0:T(8,128)(2,1)S(1)}, bf16[256,2048]{1,0:T(8,128)(2,1)S(1)}) custom-call(bf16[256,2816]{1,0:T(8,128)(2,1)S(1)} %reshape.44.rows_ref, bf16[512,768]{1,0:T(8,128)(2,1)S(1)} %copy-done.4, bf16[512,768]{1,0:T(8,128)(2,1)} %collective-permute-done.refs_1_, bf16[512,768]{1,0:T(8,128)(2,1)} %collective-permute-done.2.refs_2_, ...), custom_call_target="tpu_custom_call" | custom-call | flops 3221225472 | bytes 9175040 | tf_op jit(solution)/shard_map/pallas_call | solution.py:56
  191.9 11.4 %all-to-all-start.2 = ((bf16[128,2,2048]{2,1,0:T(2,128)(2,1)}), bf16[128,2,2048]{2,1,0:T(2,128)(2,1)}, u32[]{:S(2)}, u32[]{:S(2)}) async-start(bf16[128,2,2048]{2,1,0:T(2,128)(2,1)} %reshape.45), calls=%async_computation.2 | async-start | bytes 2097152 | tf_op jit(solution)/shard_map/all_to_all | solution.py:228
  203.4 3.1 collective-permute-start.7
  206.5 3.4 collective-permute-start.9
  212.5 4.6 %collective-permute-start.8 = (bf16[256,512]{1,0:T(8,128)(2,1)S(1)}, bf16[256,512]{1,0:T(8,128)(2,1)S(1)}, u32[]{:S(2)}, u32[]{:S(2)}) collective-permute-start(bf16[256,512]{1,0:T(8,128)(2,1)S(1)} %get-tuple-element.17), channel_id=1, source_target_pairs={{0,384},{128,0},{256,128},{384,256},{1,385},{129,1},{257,129},{385... | collective-permute-start | bytes 786440 | tf_op jit(solution)/shard_map/ppermute | solution.py:13
  217.1 2.2 collective-permute-start.10
  219.3 5.4 %collective-permute-done.7 = bf16[256,1536]{1,0:T(8,128)(2,1)} collective-permute-done((bf16[256,1536]{1,0:T(8,128)(2,1)S(1)}, bf16[256,1536]{1,0:T(8,128)(2,1)}, u32[]{:S(2)}, u32[]{:S(2)}) %collective-permute-start.7) | collective-permute-done | bytes 786464 | tf_op jit(solution)/shard_map/ppermute | solution.py:13
  228.7 4.8 %collective-permute-start.12 = (bf16[128,1536]{1,0:T(8,128)(2,1)S(1)}, bf16[128,1536]{1,0:T(8,128)(2,1)S(1)}, u32[]{:S(2)}, u32[]{:S(2)}) collective-permute-start(bf16[128,1536]{1,0:T(8,128)(2,1)S(1)} %slice.49), channel_id=1, source_target_pairs={{0,384},{128,0},{256,128},{384,256},{1,385},{129,1},{257,129},{385... | collective-permute-start | bytes 1179656 | tf_op jit(solution)/shard_map/ppermute | solution.py:13
  238.1 6.6 %collective-permute-done.11 = bf16[128,1536]{1,0:T(8,128)(2,1)S(1)} collective-permute-done((bf16[128,1536]{1,0:T(8,128)(2,1)S(1)}, bf16[128,1536]{1,0:T(8,128)(2,1)S(1)}, u32[]{:S(2)}, u32[]{:S(2)}) %collective-permute-start.11) | collective-permute-done | bytes 393248 | tf_op jit(solution)/shard_map/ppermute | solution.py:13
  248.5 3.6 %reshape.47 = bf16[128,4,2,768]{3,2,1,0:T(2,128)(2,1)S(1)} reshape(bf16[512,1536]{1,0:T(8,128)(2,1)} %add_convert_fusion) | data formatting | bytes 3145728 | tf_op jit(solution)/shard_map/reshape | solution.py:256
  252.8 89.8 %shard_map.78 = bf16[128,2,4,768]{3,2,1,0:T(4,128)(2,1)S(1)} custom-call(bf16[128,2,4,768]{3,2,1,0:T(4,128)(2,1)S(1)} %bitcast.26), custom_call_target="tpu_custom_call" | custom-call | tf_op jit(solution)/shard_map/pallas_call | solution.py:163
  (66 shorter events, 36.1 us)
Async XLA Ops:
  5.4 20.7 %copy-start.8 = (s32[128,1]{0,1:T(1,128)S(1)}, s32[128,1]{0,1:T(1,128)}, u32[]{:S(2)}) copy-start(s32[128,1]{0,1:T(1,128)} %param.9) | copy-start | bytes 1540
  5.4 21.2 %copy-start.7 = (bf16[128,1,768]{2,0,1:T(8,128)(2,1)S(1)}, bf16[128,1,768]{2,0,1:T(8,128)(2,1)}, u32[]{:S(2)}) copy-start(bf16[128,1,768]{2,0,1:T(8,128)(2,1)} %param.7) | copy-start | bytes 589828
  5.4 21.2 %copy-start.10 = (f32[128,1]{0,1:T(1,128)S(1)}, f32[128,1]{0,1:T(1,128)}, u32[]{:S(2)}) copy-start(f32[128,1]{0,1:T(1,128)} %param.8) | copy-start | bytes 1540
  5.4 21.3 %copy-start.6 = (bf16[128,2048]{1,0:T(8,128)(2,1)S(1)}, bf16[128,2048]{1,0:T(8,128)(2,1)}, u32[]{:S(2)}) copy-start(bf16[128,2048]{1,0:T(8,128)(2,1)} %param.6) | copy-start | bytes 1572868
  5.4 93.7 %all-to-all-start = ((bf16[128,2,4,768]{3,2,1,0:T(4,128)(2,1)}), bf16[128,2,4,768]{3,2,1,0:T(4,128)(2,1)S(1)}, u32[]{:S(2)}, u32[]{:S(2)}) async-start(bf16[128,2,4,768]{3,2,1,0:T(4,128)(2,1)} %copy.20), calls=%async_computation | async-start | bytes 3145728 | tf_op jit(solution)/shard_map/all_to_all | solution.py:196
  99.1 79.7 %all-to-all-start.1 = ((bf16[128,2,2816]{2,1,0:T(2,128)(2,1)}), bf16[128,2,2816]{2,1,0:T(2,128)(2,1)}, u32[]{:S(2)}, u32[]{:S(2)}) async-start(bf16[128,2,2816]{2,1,0:T(2,128)(2,1)} %reshape.43), calls=%async_computation.1 | async-start | bytes 2883584 | tf_op jit(solution)/shard_map/all_to_all | solution.py:223
  112.8 4.8 %copy-start.5 = (bf16[128,1,4,768]{3,2,1,0:T(4,128)(2,1)S(1)}, bf16[128,1,4,768]{3,2,1,0:T(4,128)(2,1)}, u32[]{:S(2)}) copy-start(bf16[128,1,4,768]{3,2,1,0:T(4,128)(2,1)} %get-tuple-element.14) | copy-start | bytes 2359300
  114.4 67.8 %copy-start.3 = (bf16[512,768]{1,0:T(8,128)(2,1)}, bf16[512,768]{1,0:T(8,128)(2,1)S(1)}, u32[]{:S(2)}) copy-start(bf16[512,768]{1,0:T(8,128)(2,1)S(1)} %reshape_squeeze.6.refs_0_) | copy-start | bytes 2359300
  114.4 21.4 %collective-permute-start.1 = (bf16[512,768]{1,0:T(8,128)(2,1)S(1)}, bf16[512,768]{1,0:T(8,128)(2,1)}, u32[]{:S(2)}, u32[]{:S(2)}) collective-permute-start(bf16[512,768]{1,0:T(8,128)(2,1)S(1)} %reshape_squeeze.6.refs_0_), channel_id=1, source_target_pairs={{0,128},{128,256},{256,384},{384,0},{1,129},{129,257},{257,385},{3... | collective-permute-start | bytes 2359304 | tf_op jit(solution)/shard_map/ppermute | solution.py:13
  118.6 20.1 %collective-permute-start.3 = (bf16[512,768]{1,0:T(8,128)(2,1)}, bf16[512,768]{1,0:T(8,128)(2,1)}, u32[]{:S(2)}, u32[]{:S(2)}) collective-permute-start(bf16[512,768]{1,0:T(8,128)(2,1)} %reshape_squeeze.7.refs_4_), channel_id=1, source_target_pairs={{0,384},{128,0},{256,128},{384,256},{1,385},{129,1},{257,129},{385... | collective-permute-start | bytes 2359304 | tf_op jit(solution)/shard_map/ppermute | solution.py:13
  122.0 60.2 %collective-permute-start = (bf16[512,768]{1,0:T(8,128)(2,1)S(1)}, bf16[512,768]{1,0:T(8,128)(2,1)}, u32[]{:S(2)}, u32[]{:S(2)}) collective-permute-start(bf16[512,768]{1,0:T(8,128)(2,1)S(1)} %reshape_squeeze.6.refs_0_), channel_id=1, source_target_pairs={{0,384},{128,0},{256,128},{384,256},{1,385},{129,1},{257,129},{385... | collective-permute-start | bytes 2359304 | tf_op jit(solution)/shard_map/ppermute | solution.py:13
  125.2 57.1 %collective-permute-start.5 = (bf16[512,768]{1,0:T(8,128)(2,1)}, bf16[512,768]{1,0:T(8,128)(2,1)}, u32[]{:S(2)}, u32[]{:S(2)}) collective-permute-start(bf16[512,768]{1,0:T(8,128)(2,1)} %reshape_squeeze.7.refs_4_), channel_id=1, source_target_pairs={{0,128},{128,256},{256,384},{384,0},{1,129},{129,257},{257,385},{3... | collective-permute-start | bytes 2359304 | tf_op jit(solution)/shard_map/ppermute | solution.py:13
  135.8 46.5 %collective-permute-start.2 = (bf16[512,768]{1,0:T(8,128)(2,1)}, bf16[512,768]{1,0:T(8,128)(2,1)}, u32[]{:S(2)}, u32[]{:S(2)}) collective-permute-start(bf16[512,768]{1,0:T(8,128)(2,1)} %collective-permute-done.1.refs_3_), channel_id=1, source_target_pairs={{0,128},{128,256},{256,384},{384,0},{1,129},{129,257},{257,385},{3... | collective-permute-start | bytes 2359304 | tf_op jit(solution)/shard_map/ppermute | solution.py:13
  138.7 43.6 %collective-permute-start.4 = (bf16[512,768]{1,0:T(8,128)(2,1)}, bf16[512,768]{1,0:T(8,128)(2,1)}, u32[]{:S(2)}, u32[]{:S(2)}) collective-permute-start(bf16[512,768]{1,0:T(8,128)(2,1)} %collective-permute-done.3.refs_5_), channel_id=1, source_target_pairs={{0,384},{128,0},{256,128},{384,256},{1,385},{129,1},{257,129},{385... | collective-permute-start | bytes 2359304 | tf_op jit(solution)/shard_map/ppermute | solution.py:13
  191.9 11.4 %copy-start.2 = (bf16[256,1536]{1,0:T(8,128)(2,1)S(1)}, bf16[256,1536]{1,0:T(8,128)(2,1)}, u32[]{:S(2)}) copy-start(bf16[256,1536]{1,0:T(8,128)(2,1)} %copy-done.1) | copy-start | bytes 2359300
  191.9 152.7 %all-to-all-start.2 = ((bf16[128,2,2048]{2,1,0:T(2,128)(2,1)}), bf16[128,2,2048]{2,1,0:T(2,128)(2,1)}, u32[]{:S(2)}, u32[]{:S(2)}) async-start(bf16[128,2,2048]{2,1,0:T(2,128)(2,1)} %reshape.45), calls=%async_computation.2 | async-start | bytes 2097152 | tf_op jit(solution)/shard_map/all_to_all | solution.py:228
  203.4 21.3 %collective-permute-start.7 = (bf16[256,1536]{1,0:T(8,128)(2,1)S(1)}, bf16[256,1536]{1,0:T(8,128)(2,1)}, u32[]{:S(2)}, u32[]{:S(2)}) collective-permute-start(bf16[256,1536]{1,0:T(8,128)(2,1)S(1)} %copy-done.2), channel_id=1, source_target_pairs={{0,128},{128,256},{256,384},{384,0},{1,129},{129,257},{257,385},{3... | collective-permute-start | bytes 2359304 | tf_op jit(solution)/shard_map/ppermute | solution.py:13
  206.5 21.2 %collective-permute-start.9 = (bf16[256,1536]{1,0:T(8,128)(2,1)S(1)}, bf16[256,1536]{1,0:T(8,128)(2,1)}, u32[]{:S(2)}, u32[]{:S(2)}) collective-permute-start(bf16[256,1536]{1,0:T(8,128)(2,1)S(1)} %copy-done.2), channel_id=1, source_target_pairs={{0,384},{128,0},{256,128},{384,256},{1,385},{129,1},{257,129},{385... | collective-permute-start | bytes 2359304 | tf_op jit(solution)/shard_map/ppermute | solution.py:13
  210.0 23.5 %collective-permute-start.6 = (bf16[256,512]{1,0:T(8,128)(2,1)S(1)}, bf16[256,512]{1,0:T(8,128)(2,1)S(1)}, u32[]{:S(2)}, u32[]{:S(2)}) collective-permute-start(bf16[256,512]{1,0:T(8,128)(2,1)S(1)} %get-tuple-element.18), channel_id=1, source_target_pairs={{0,128},{128,256},{256,384},{384,0},{1,129},{129,257},{257,385},{3... | collective-permute-start | bytes 786440 | tf_op jit(solution)/shard_map/ppermute | solution.py:13
  212.5 22.7 %collective-permute-start.8 = (bf16[256,512]{1,0:T(8,128)(2,1)S(1)}, bf16[256,512]{1,0:T(8,128)(2,1)S(1)}, u32[]{:S(2)}, u32[]{:S(2)}) collective-permute-start(bf16[256,512]{1,0:T(8,128)(2,1)S(1)} %get-tuple-element.17), channel_id=1, source_target_pairs={{0,384},{128,0},{256,128},{384,256},{1,385},{129,1},{257,129},{385... | collective-permute-start | bytes 786440 | tf_op jit(solution)/shard_map/ppermute | solution.py:13
  217.1 21.1 %collective-permute-start.10 = (bf16[256,512]{1,0:T(8,128)(2,1)S(1)}, bf16[256,512]{1,0:T(8,128)(2,1)S(1)}, u32[]{:S(2)}, u32[]{:S(2)}) collective-permute-start(bf16[256,512]{1,0:T(8,128)(2,1)S(1)} %get-tuple-element.16), channel_id=1, source_target_pairs={{0,256},{128,384},{256,0},{384,128},{1,257},{129,385},{257,1},{385... | collective-permute-start | bytes 786440 | tf_op jit(solution)/shard_map/ppermute | solution.py:13
  225.7 19.0 %collective-permute-start.11 = (bf16[128,1536]{1,0:T(8,128)(2,1)S(1)}, bf16[128,1536]{1,0:T(8,128)(2,1)S(1)}, u32[]{:S(2)}, u32[]{:S(2)}) collective-permute-start(bf16[128,1536]{1,0:T(8,128)(2,1)S(1)} %slice.47), channel_id=1, source_target_pairs={{0,128},{128,256},{256,384},{384,0},{1,129},{129,257},{257,385},{3... | collective-permute-start | bytes 1179656 | tf_op jit(solution)/shard_map/ppermute | solution.py:13
  228.7 17.6 %collective-permute-start.12 = (bf16[128,1536]{1,0:T(8,128)(2,1)S(1)}, bf16[128,1536]{1,0:T(8,128)(2,1)S(1)}, u32[]{:S(2)}, u32[]{:S(2)}) collective-permute-start(bf16[128,1536]{1,0:T(8,128)(2,1)S(1)} %slice.49), channel_id=1, source_target_pairs={{0,384},{128,0},{256,128},{384,256},{1,385},{129,1},{257,129},{385... | collective-permute-start | bytes 1179656 | tf_op jit(solution)/shard_map/ppermute | solution.py:13
  252.8 89.8 %copy-start.9 = (s32[128]{0:T(128)S(1)}, s32[128]{0:T(128)}, u32[]{:S(2)}) copy-start(s32[128]{0:T(128)} %param.10) | copy-start | bytes 1540
  (3 other events, 3.2 us)
